TPU v7x, 512 devices: a whole 4x8x8 slice. The times are simulated.
512 devices in a mesh: tm: 32 (over y, z_lo, core), chan: 16 (over z_hi, x).
Axes of the slice: x: 4, y: 8, z: 8 (z_hi: 4, z_lo: 2; z = z_hi * 2 + z_lo), core: 2. Of those that a mesh axis runs over, the one named last changes fastest.
Arguments:
- record: bfloat16 [2048, 49152], P('chan', 'tm'), may hold values from -250 to 250
- offsets: int32 [4], replicated, may hold values from 0 to 37152, as said below
- dead_mask: int32 [2048], P('chan'), may hold values 0 or 1
- sources: int32 [128], replicated, may hold values from 0 to 2047
Outputs:
- cross_spectra: float32 [640, 2, 128, 2048], P('tm', None, None, 'chan')
Inputs may be any that keep to these rules, and one draw needn't show every extreme that they name: offsets[w] lies between w * 12000 and w * 12000 + 49152 - 4 * 12000; offsets[0] is 0 and the last window ends at the record's last sample.
All inputs are finite; a program needn't handle non-finite values. No bound on the sum of `dead_mask` on one device may be relied on, other than what follows from the above.
Results may differ from a plain program's by a relative error of at most 0.002.
The roundings to bfloat16 on the way count: a program that leaves them out, or rounds other values in their place, can miss the bound.
Values may be sent and summed in bfloat16 or wider, within the bound.
A program may use at most 128 MiB of HBM per device.

v0:
```python
import math

import jax
import jax.numpy as jnp
from jax import lax
from jax.sharding import PartitionSpec as P

W = 12000
F = 640
FLO = 6
NWIN = 4


def band_basis(first_bin, width, times):
    bins = first_bin + jnp.arange(width, dtype=jnp.int32)
    phase = times[:, None] * bins[None, :] % W
    angle = phase.astype(jnp.float32) * (2.0 * math.pi / W)
    return jnp.stack([jnp.cos(angle), -jnp.sin(angle)], axis=-1)


def amplitude(fourier_coefficients):
    return jnp.sqrt(fourier_coefficients[:, :, 0] ** 2 + fourier_coefficients[:, :, 1] ** 2)


def whiten(fourier_coefficients, magnitude, level):
    denominator = magnitude + 0.1 * level[None] + 1e-06
    return (fourier_coefficients / denominator[:, :, None, :]).astype(jnp.bfloat16)


def shards(record, offsets, dead_mask, sources):
    tm_count = lax.axis_size("tm")
    bins_dev = F // tm_count
    channels = record.shape[0]
    group_first = lax.axis_index("tm") * record.shape[1]
    local_times = group_first + jnp.arange(record.shape[1], dtype=jnp.int32)
    start = jnp.int32(0)
    blocks = []
    for first in range(0, lax.axis_size("tm") * bins_dev, 64):
        width = min(64, lax.axis_size("tm") * bins_dev - first)
        per_window = []
        for window in range(NWIN):
            shifted = local_times - offsets[window]
            inside = (shifted >= 0) & (shifted < W)
            basis = band_basis(FLO + start + first, width, jnp.where(inside, shifted, 0))
            basis = (basis * inside[:, None, None].astype(jnp.float32)).astype(jnp.bfloat16)
            per_window.append(
                jnp.einsum("ct,tfp->fpc", record, basis, preferred_element_type=jnp.float32)
            )
        blocks.append(jnp.stack(per_window, axis=1))
    fourier_coefficients = lax.psum_scatter(
        jnp.concatenate(blocks, axis=0), "tm", scatter_dimension=0, tiled=True
    )
    magnitude = amplitude(fourier_coefficients)
    level = lax.psum(jnp.sum(magnitude, axis=0), "tm") / F
    white = whiten(fourier_coefficients, magnitude, level)
    white = white * dead_mask.astype(jnp.bfloat16)[None, None, None, :]
    local_index = sources - lax.axis_index("chan") * channels
    onehot = (jnp.arange(channels, dtype=jnp.int32)[:, None] == local_index[None, :]).astype(
        jnp.bfloat16
    )
    selected_bins = jnp.einsum("fwpc,cs->fwps", white, onehot, preferred_element_type=jnp.float32)
    source_spec = lax.psum(selected_bins.astype(jnp.bfloat16), "chan")
    left_channel = source_spec.reshape(bins_dev, NWIN * 2, source_spec.shape[3])
    right_channel_real = white.reshape(bins_dev, NWIN * 2, channels)
    right_channel_imaginary = jnp.concatenate(
        [white[:, :, 1:2], -white[:, :, 0:1]], axis=2
    ).reshape(bins_dev, NWIN * 2, channels)
    real_component = jnp.einsum(
        "qia,qie->qae", left_channel, right_channel_real, preferred_element_type=jnp.float32
    )
    imaginary_component = jnp.einsum(
        "qia,qie->qae", left_channel, right_channel_imaginary, preferred_element_type=jnp.float32
    )
    return jnp.stack([real_component, imaginary_component], axis=1) / NWIN


def solution(mesh):
    return jax.shard_map(
        shards,
        mesh=mesh,
        in_specs=(P("chan", "tm"), P(), P("chan"), P()),
        out_specs=P("tm", None, None, "chan"),
        check_vma=False,
    )
```

profile of v0, /device:TPU:32, one launch (start us, length us, event | category | flops | bytes accessed | tf_op | source)
XLA Modules:
  0.0 483.6 jit_solution(6104584640488371410)
XLA Ops:
  6.5 0.0 copy-start
  6.5 0.0 all-reduce.3.cloned.1.call-start
  6.6 1.5 fusion.474
  8.1 1.3 fusion.412
  9.4 1.3 fusion.428
  10.7 1.2 fusion.418
  12.0 1.2 fusion.430
  13.3 64.1 %fusion.202 = (f32[1536,64,1]{0,1,2:T(8,128)S(1)}, f32[1536,64,1]{0,1,2:T(8,128)S(1)}, f32[1536,64,1]{0,1,2:T(8,128)S(1)}, f32[1536,64,1]{0,1,2:T(8,128)S(1)}, f...) fusion(s32[64]{0:T(128)S(1)} %get-tuple-element.231, ...), kind=kLoop, calls=%fused_computation.288 | loop fusion | flops 39321600 | bytes 31484416 | tf_op jit(solution)/shard_map/cos | solution.py:18
  77.4 0.3 convolution_bitcast_fusion.5
  77.7 0.3 convolution_bitcast_fusion.9
  77.9 0.3 convolution_bitcast_fusion.4
  78.2 0.3 convolution_bitcast_fusion.8
  78.5 0.3 convolution_bitcast_fusion.3
  78.8 0.3 convolution_bitcast_fusion.7
  79.0 0.3 convolution_bitcast_fusion.2
  79.3 0.3 convolution_bitcast_fusion.6
  79.6 0.3 convolution_bitcast_fusion.13
  79.8 0.3 convolution_bitcast_fusion.12
  80.1 0.3 convolution_bitcast_fusion.11
  80.4 0.3 convolution_bitcast_fusion.10
  80.6 0.3 convolution_bitcast_fusion.17
  80.9 0.3 convolution_bitcast_fusion.16
  81.2 0.3 convolution_bitcast_fusion.15
  81.5 0.3 convolution_bitcast_fusion.14
  81.7 0.3 convolution_bitcast_fusion.21
  82.0 0.3 convolution_bitcast_fusion.20
  82.3 0.3 convolution_bitcast_fusion.19
  82.5 0.3 convolution_bitcast_fusion.18
  82.8 0.3 convolution_bitcast_fusion.25
  83.1 0.3 convolution_bitcast_fusion.24
  83.3 0.3 convolution_bitcast_fusion.23
  83.6 0.3 convolution_bitcast_fusion.22
  83.9 0.3 convolution_bitcast_fusion.29
  84.2 0.3 convolution_bitcast_fusion.28
  84.4 0.3 convolution_bitcast_fusion.27
  84.7 0.3 convolution_bitcast_fusion.26
  85.0 0.3 convolution_bitcast_fusion.33
  85.2 0.3 convolution_bitcast_fusion.32
  85.5 0.3 convolution_bitcast_fusion.31
  85.8 0.3 convolution_bitcast_fusion.30
  86.0 0.3 convolution_bitcast_fusion.37
  86.3 0.3 convolution_bitcast_fusion.36
  86.6 0.3 convolution_bitcast_fusion.35
  86.8 0.3 convolution_bitcast_fusion.34
  87.1 0.3 convolution_bitcast_fusion.41
  87.4 0.3 convolution_bitcast_fusion.40
  87.7 0.3 convolution_bitcast_fusion.39
  87.9 0.3 convolution_bitcast_fusion.38
  88.5 3.2 copy.14
  91.7 0.0 all-reduce.3.cloned.1.call-update
  91.7 0.6 copy-done.1
  92.3 1.3 dynamic-slice
  94.4 0.0 copy-done.2
  94.4 238.8 %all-reduce.3.cloned.1.call-done = f32[640,4,2,128]{3,1,2,0:T(4,128)} async-done(((f32[640,4,2,128]{3,1,2,0:T(4,128)}), f32[640,4,2,128]{3,1,2,0:T(4,128)}) %all-reduce.3.cloned.1.call-update) | async-done | bytes 2621456
  333.2 0.8 fusion.472
  334.0 55.1 %psum.14 = f32[4,128]{1,0:T(4,128)S(1)} all-reduce(f32[4,128]{1,0:T(4,128)S(1)} %fusion.472), channel_id=1, replica_groups=mesh['tm'=32,'chan'=16] {'tm'}, use_global_device_ids=true, to_apply=%region_2.3 | all-reduce | flops 512 | bytes 4096 | tf_op jit(solution)/shard_map/psum | solution.py:54
  389.2 0.8 add_bitcast_fusion
  390.0 0.9 fusion.406
  391.0 0.2 convolution_convert_fusion
  391.2 82.7 %psum.15 = bf16[20,8,128]{2,1,0:T(8,128)(2,1)S(1)} all-reduce(bf16[20,8,128]{2,1,0:T(8,128)(2,1)S(1)} %copy.16), channel_id=1, replica_groups=mesh['tm'=32,'chan'=16] {'chan'}, use_global_device_ids=true, to_apply=%region_3.4 | all-reduce | flops 20480 | bytes 81920 | tf_op jit(solution)/shard_map/psum | solution.py:62
  473.9 0.4 convolution_bitcast_fusion.1
  474.3 0.4 convolution_bitcast_fusion
  474.7 0.3 maximum_multiply_fusion
  475.0 1.7 copy.19
  (26 shorter events, 0.4 us)
Async XLA Ops:
  6.5 70.8 %copy-start = (bf16[128,1536]{1,0:T(8,128)(2,1)S(1)}, bf16[128,1536]{1,0:T(8,128)(2,1)}, u32[]{:S(2)}) copy-start(bf16[128,1536]{1,0:T(8,128)(2,1)} %param.4) | copy-start | bytes 1179652
  6.5 326.7 %all-reduce.3.cloned.1.call-start = ((), (), s32[]{:S(2)}) async-start(), calls=%async_computation | async-start | bytes 5242880
  91.7 0.7 copy-start.1
  91.7 2.7 copy-start.2
Sparse Core Ops, SparseCore 0:
  91.8 241.3 all-reduce.2
where the time goes:
time: 484 us
  waiting for transfers between devices  239 us (49%)
  blocking collectives  138 us (29%)
  other arithmetic  72.5 us (15%)
  between operations  14.6 us (3%)
  matrix products  11.5 us (2%)
  local copies, waits for them, and re-layouts  8.37 us (2%)
    unnamed x2, waiting for transfers between devices  239 us
    psum x1, blocking collectives, shards(): source_spec = lax.psum(selected_bins.astype(jnp.bfloat16), 'chan')  82.7 us
    cos x1, other arithmetic, band_basis(): return jnp.stack([jnp.cos(angle), -jnp.sin(angle)], axis=-1)  64.1 us
    psum x1, blocking collectives, shards(): level = lax.psum(jnp.sum(magnitude, axis=0), 'tm') / F  55.1 us
    dot_general x40, matrix products, shards(): jnp.einsum('ct,tfp->fpc', record, basis, preferred_element_type=jnp.float32)  10.5 us
  transfers between devices with their start and end apart: 1, of which 1 were waited for; matrix products, arithmetic and copies ran while one was open for 0% of the time, Pallas kernels for 0%

commit v1 on v0

v1 whole, which is shorter than its diff:
```python
import functools
import math

import jax
import jax.numpy as jnp
from jax import lax
from jax.experimental import pallas as pl
from jax.experimental.pallas import tpu as pltpu
from jax.sharding import PartitionSpec as P

W = 12000
F = 640
FLO = 6
NWIN = 4
SLOTS = 2
FA = 64

MESH = pl.DeviceIdType.MESH


def _exchange_kernel(axis, n, gather, x_ref, o_ref, send_sem, recv_sem):
    me = lax.axis_index(axis)
    barrier = pltpu.get_barrier_semaphore()
    for i in range(1, n):
        peer = lax.rem(me + i, n)
        pl.semaphore_signal(barrier, inc=1, device_id={axis: peer}, device_id_type=MESH)
    pl.semaphore_wait(barrier, n - 1)

    def src_block(peer):
        return x_ref if gather else x_ref.at[peer]

    copies = []
    for i in range(1, n):
        peer = lax.rem(me + i, n)
        copy = pltpu.make_async_remote_copy(
            src_ref=src_block(peer),
            dst_ref=o_ref.at[me],
            send_sem=send_sem.at[peer],
            recv_sem=recv_sem.at[me],
            device_id={axis: peer},
            device_id_type=MESH,
        )
        copy.start()
        copies.append(copy)
    if gather:
        o_ref[me] = x_ref[...]
    else:
        o_ref[me] = x_ref[me]
    for copy in copies:
        copy.wait_send()
    for i in range(1, n):
        src = lax.rem(me + n - i, n)
        pltpu.make_async_remote_copy(
            src_ref=src_block(src),
            dst_ref=o_ref.at[src],
            send_sem=send_sem.at[src],
            recv_sem=recv_sem.at[src],
            device_id={axis: src},
            device_id_type=MESH,
        ).wait_recv()


def exchange(x, axis, n, gather, collective_id):
    out_shape = (n,) + (x.shape if gather else x.shape[1:])
    return pl.pallas_call(
        functools.partial(_exchange_kernel, axis, n, gather),
        out_shape=jax.ShapeDtypeStruct(out_shape, x.dtype),
        in_specs=[pl.BlockSpec(memory_space=pltpu.VMEM)],
        out_specs=pl.BlockSpec(memory_space=pltpu.VMEM),
        scratch_shapes=[pltpu.SemaphoreType.DMA((n,)), pltpu.SemaphoreType.DMA((n,))],
        compiler_params=pltpu.CompilerParams(collective_id=collective_id, has_side_effects=True),
    )(x)


def phasor(times, bins):
    phase = times[:, None] * bins[None, :] % W
    angle = phase.astype(jnp.float32) * (2.0 * math.pi / W)
    return jnp.cos(angle), -jnp.sin(angle)


def band_basis(times):
    coarse = FLO + FA * jnp.arange(F // FA, dtype=jnp.int32)
    fine = jnp.arange(FA, dtype=jnp.int32)
    ar, ai = phasor(times, coarse)
    br, bi = phasor(times, fine)
    ar, ai = ar[:, :, None], ai[:, :, None]
    br, bi = br[:, None, :], bi[:, None, :]
    re = ar * br - ai * bi
    im = ar * bi + ai * br
    basis = jnp.stack([re, im], axis=-1).reshape(times.shape[0], F, 2)
    return basis.astype(jnp.bfloat16)


def first_window(offsets, start):
    return jnp.sum((offsets + W <= start).astype(jnp.int32))


def shards(record, offsets, dead_mask, sources):
    n_tm = lax.axis_size("tm")
    n_chan = lax.axis_size("chan")
    bins_dev = F // n_tm
    channels, span = record.shape
    me = lax.axis_index("tm")
    start = me * span
    local_times = start + jnp.arange(span, dtype=jnp.int32)
    wa = first_window(offsets, start)

    partials = []
    for slot in range(SLOTS):
        window = wa + slot
        origin = offsets[jnp.minimum(window, NWIN - 1)]
        shifted = local_times - origin
        inside = (shifted >= 0) & (shifted < W) & (window < NWIN)
        basis = band_basis(jnp.where(inside, shifted, 0))
        masked = jnp.where(inside[None, :], record, jnp.zeros_like(record))
        partials.append(
            jnp.einsum("tkp,ct->kpc", basis, masked, preferred_element_type=jnp.float32)
        )
    blocks = jnp.stack(partials, axis=1).reshape(n_tm, bins_dev * SLOTS * 2, channels)
    received = exchange(blocks, "tm", n_tm, False, 0).reshape(
        n_tm, bins_dev, SLOTS, 2, channels
    )
    src_start = jnp.arange(n_tm, dtype=jnp.int32) * span
    src_wa = jnp.sum((offsets[None, :] + W <= src_start[:, None]).astype(jnp.int32), axis=1)
    src_win = src_wa[:, None] + jnp.arange(SLOTS, dtype=jnp.int32)[None, :]
    route = (src_win[None] == jnp.arange(NWIN, dtype=jnp.int32)[:, None, None]).astype(
        jnp.float32
    )
    spectrum = jnp.einsum(
        "wsj,skjpc->kwpc", route, received, precision=lax.Precision.HIGHEST
    )

    magnitude = jnp.sqrt(spectrum[:, :, 0] ** 2 + spectrum[:, :, 1] ** 2)
    level_part = jnp.sum(magnitude, axis=0)
    level_part = jnp.concatenate([level_part, jnp.zeros_like(level_part)], axis=0)
    level = jnp.sum(exchange(level_part, "tm", n_tm, True, 1), axis=0)[:NWIN] / F
    denominator = magnitude + 0.1 * level[None] + 1e-06
    white = (spectrum / denominator[:, :, None, :]).astype(jnp.bfloat16)
    white = white * dead_mask.astype(jnp.bfloat16)[None, None, None, :]

    local_index = sources - lax.axis_index("chan") * channels
    onehot = (jnp.arange(channels, dtype=jnp.int32)[:, None] == local_index[None, :]).astype(
        jnp.bfloat16
    )
    contrib = jnp.einsum("kwpc,cs->kwps", white, onehot, preferred_element_type=jnp.float32)
    contrib = contrib.astype(jnp.bfloat16).reshape(bins_dev * NWIN * 2, sources.shape[0])
    gathered = exchange(contrib, "chan", n_chan, True, 2)
    source_spec = jnp.sum(gathered.astype(jnp.float32), axis=0).astype(jnp.bfloat16)

    left_channel = source_spec.reshape(bins_dev, NWIN * 2, sources.shape[0])
    right_channel_real = white.reshape(bins_dev, NWIN * 2, channels)
    right_channel_imaginary = jnp.concatenate(
        [white[:, :, 1:2], -white[:, :, 0:1]], axis=2
    ).reshape(bins_dev, NWIN * 2, channels)
    real_component = jnp.einsum(
        "qia,qie->qae", left_channel, right_channel_real, preferred_element_type=jnp.float32
    )
    imaginary_component = jnp.einsum(
        "qia,qie->qae", left_channel, right_channel_imaginary, preferred_element_type=jnp.float32
    )
    return jnp.stack([real_component, imaginary_component], axis=1) / NWIN


def solution(mesh):
    return jax.shard_map(
        shards,
        mesh=mesh,
        in_specs=(P("chan", "tm"), P(), P("chan"), P()),
        out_specs=P("tm", None, None, "chan"),
        check_vma=False,
    )
```

time: 484 us -> 112 us (0.23)
  the two profiles are of different devices: /device:TPU:32 before, /device:TPU:22 now
where the time goes in v1:
time: 112 us; the launch traced here: 111 us
  Pallas kernels  84.2 us (75%)
  other arithmetic  12.9 us (12%)
  local copies, waits for them, and re-layouts  6.48 us (6%)
  matrix products  5.5 us (5%)
  between operations  2.18 us (2%)
    pallas_call x3, Pallas kernels, exchange(): pl.pallas_call(functools.partial(_exchange_kernel, axis, n, gather), out_...  84.2 us
    cos x3, other arithmetic, phasor(): return (jnp.cos(angle), -jnp.sin(angle))  4.09 us
    dot_general x2, matrix products, shards(): jnp.einsum('tkp,ct->kpc', basis, masked, preferred_element_type=jnp.float32)  2.4 us

profile of v1, /device:TPU:22, one launch (start us, length us, event | category | flops | bytes accessed | tf_op | source)
XLA Modules:
  0.0 111.3 jit_solution(13210573072335217040)
XLA Ops:
  0.0 1.3 %broadcast_add_fusion = (s32[4]{0:T(128)S(1)}, s32[]{:T(128)}) fusion(s32[4]{0:T(128)} %param.5, s32[]{:T(128)S(6)} %mul.321), kind=kLoop, calls=%fused_computation.105 | loop fusion | flops 15 | bytes 40 | tf_op jit(solution)/shard_map/add | solution.py:95
  2.6 1.4 %fusion.82 = (s32[1]{0:T(128)}, s32[1]{0:T(128)}) fusion(s32[4]{0:T(128)} %param.5, s32[]{:T(128)S(6)} %select_n.77, s32[]{:T(128)S(6)} %select_n.82), kind=kLoop, calls=%fused_computation.112 | loop fusion | bytes 24 | tf_op jit(solution)/shard_map/dynamic_slice | solution.py:111
  4.7 1.3 %fusion.62 = (s32[1536]{0:T(1024)S(1)}, s32[1536]{0:T(1024)S(1)}) fusion(s32[]{:T(128)} %bitcast, s32[]{:T(128)S(6)} %mul.321, pred[]{:T(512)S(6)} %lt.56, pred[]{:T(512)S(6)} %lt.61, s32[]{:T(128)} %bitcast.5), kind=kLoop, calls=%fused_computation.84 | loop fusion | flops 19968 | bytes 12302 | tf_op jit(solution)/shard_map/jit(_where)/select_n | solution.py:114
  5.9 1.6 %fusion.32 = (f32[1536,64]{0,1:T(8,128)S(1)}, f32[1536,64]{0,1:T(8,128)S(1)}) fusion(s32[1536]{0:T(1024)S(1)} %get-tuple-element.25), kind=kLoop, calls=%fused_computation.41 | loop fusion | flops 983040 | bytes 792576 | tf_op jit(solution)/shard_map/cos | solution.py:78
  7.5 0.0 copy-start
  7.6 0.9 fusion.48
  8.4 1.1 subtract_convert_fusion.1
  9.5 1.3 %fusion.69 = (pred[1536]{0:T(1024)(128)(4,1)S(1)}, pred[1536]{0:T(1024)(128)(4,1)S(1)}) fusion(s32[]{:T(128)} %bitcast.5, s32[]{:T(128)S(6)} %mul.321, pred[]{:T(512)S(6)} %lt.61, pred[]{:T(512)S(6)} %lt.56, s32[]{:T(128)} %bitcast), kind=kLoop, calls=%fused_computation.91 | loop fusion | flops 16896 | bytes 3086 | tf_op jit(solution)/shard_map/and | solution.py:113
  10.8 0.0 copy-done
  10.8 1.2 %fusion.13 = f32[640,1,2,128]{3,0,2,1:T(8,128)S(1)} fusion(bf16[1536,640,1]{0,1,2:T(8,128)(2,1)S(1)} %bitcast.52, bf16[1536,640,1]{0,1,2:T(8,128)(2,1)S(1)} %bitcast.51, bf16[128,1536]{1,0:T(8,128)(2,1)S(1)} %copy-done, pred[1536]{0:T(1024)(128)(4,1)S(1)} %get-tuple-element.28), kind=kOutput, calls=%fused_computation.19 | convolution fusion | flops 505479168 | bytes 4982272 | tf_op jit(solution)/shard_map/tkp,ct->kpc/dot_general | solution.py:117
  12.0 1.6 %fusion.28 = (f32[1536,64]{0,1:T(8,128)S(1)}, f32[1536,64]{0,1:T(8,128)S(1)}) fusion(s32[1536]{0:T(1024)S(1)} %get-tuple-element.26), kind=kLoop, calls=%fused_computation.35 | loop fusion | flops 983040 | bytes 792576 | tf_op jit(solution)/shard_map/cos | solution.py:78
  13.6 1.1 subtract_convert_fusion
  14.7 1.2 %fusion.10 = f32[640,1,2,128]{3,0,2,1:T(8,128)S(1)} fusion(bf16[1536,640,1]{0,1,2:T(8,128)(2,1)S(1)} %bitcast.54, bf16[1536,640,1]{0,1,2:T(8,128)(2,1)S(1)} %bitcast.53, bf16[128,1536]{1,0:T(8,128)(2,1)S(1)} %copy-done, pred[1536]{0:T(1024)(128)(4,1)S(1)} %get-tuple-element.27), kind=kOutput, calls=%fused_computation.18 | convolution fusion | flops 505479168 | bytes 4982272 | tf_op jit(solution)/shard_map/tkp,ct->kpc/dot_general | solution.py:117
  15.9 0.1 pad_maximum_fusion
  16.0 2.1 %copy.17 = f32[640,2,2,128]{3,2,1,0:T(2,128)} copy(f32[640,2,2,128]{3,0,2,1:T(8,128)S(1)} %pad_maximum_fusion) | data formatting | bytes 2621440 | tf_op jit(solution)/shard_map/stack | solution.py:119
  18.1 0.0 copy-start.1
  18.1 0.0 copy-start.2
  18.1 38.6 %shard_map.46 = f32[32,80,128]{2,1,0:T(8,128)} custom-call(f32[32,80,128]{2,1,0:T(8,128)} %bitcast.50), custom_call_target="tpu_custom_call" | custom-call | tf_op jit(solution)/shard_map/pallas_call | solution.py:65
  56.7 0.1 convert_reduce_fusion
  56.8 2.2 %fusion.16 = f32[20,4,2,128]{3,1,2,0:T(4,128)S(1)} fusion(f32[32,20,2,2,128]{4,3,2,1,0:T(2,128)} %bitcast.49, s32[32,2]{0,1:T(2,128)S(1)} %iota_add_fusion.1), kind=kOutput, calls=%fused_computation.20 | convolution fusion | flops 15728896 | bytes 1392896 | tf_op jit(solution)/shard_map/wsj,skjpc->kwpc/dot_general | solution.py:129
  59.0 0.6 concatenate.10.x_ref
  59.6 15.4 %shard_map.47 = f32[32,8,128]{2,1,0:T(8,128)} custom-call(f32[8,128]{1,0:T(8,128)} %concatenate.10.x_ref), custom_call_target="tpu_custom_call" | custom-call | tf_op jit(solution)/shard_map/pallas_call | solution.py:65
  74.9 0.9 reduce_sum.51
  75.9 0.0 copy-done.1
  76.0 0.0 copy-done.2
  76.0 0.2 convolution_convert_fusion
  76.2 0.7 copy.20
  76.8 30.3 %shard_map.48 = bf16[16,160,128]{2,1,0:T(8,128)(2,1)} custom-call(bf16[160,128]{1,0:T(8,128)(2,1)} %bitcast.57), custom_call_target="tpu_custom_call" | custom-call | tf_op jit(solution)/shard_map/pallas_call | solution.py:65
  107.2 1.2 %reduce_sum.52 = bf16[160,128]{1,0:T(8,128)(2,1)S(1)} reduce(bf16[16,160,128]{2,1,0:T(8,128)(2,1)} %shard_map.48, bf16[]{:T(256)} %constant.64.clone.1), dimensions={0}, to_apply=%region_4.5 | reduce | flops 307200 | bytes 696322 | tf_op jit(solution)/shard_map/reduce_sum | solution.py:148
  108.4 0.4 convolution_bitcast_fusion.1
  108.9 0.4 convolution_bitcast_fusion
  109.3 0.3 maximum_multiply_fusion
  109.6 1.7 %copy.23 = f32[20,2,128,128]{3,2,1,0:T(8,128)} copy(f32[20,2,128,128]{3,2,0,1:T(8,128)S(1)} %maximum_multiply_fusion) | data formatting | bytes 5242880 | tf_op jit(solution)/shard_map/div | solution.py:161
  (13 shorter events, 0.3 us)
Async XLA Ops:
  7.5 3.2 %copy-start = (bf16[128,1536]{1,0:T(8,128)(2,1)S(1)}, bf16[128,1536]{1,0:T(8,128)(2,1)}, u32[]{:S(2)}) copy-start(bf16[128,1536]{1,0:T(8,128)(2,1)} %param.4) | copy-start | bytes 1179652
  18.1 57.9 %copy-start.1 = (s32[128]{0:T(128)S(1)}, s32[128]{0:T(128)}, u32[]{:S(2)}) copy-start(s32[128]{0:T(128)} %param.6) | copy-start | bytes 1540
  18.1 57.9 %copy-start.2 = (s32[128]{0:T(128)S(1)}, s32[128]{0:T(128)}, u32[]{:S(2)}) copy-start(s32[128]{0:T(128)} %param.7) | copy-start | bytes 1540

commit v2 on v1

v2 whole, which is shorter than its diff:
```python
import functools
import math

import jax
import jax.numpy as jnp
from jax import lax
from jax.experimental import pallas as pl
from jax.experimental.pallas import tpu as pltpu
from jax.sharding import PartitionSpec as P

W = 12000
F = 640
FLO = 6
NWIN = 4
SLOTS = 2
FA = 64

MESH = pl.DeviceIdType.MESH


def window_plan(n_tm, span):
    total = n_tm * span
    slack = total - NWIN * W
    lows = [0] + [w * W for w in range(1, NWIN - 1)] + [total - W]
    highs = [0] + [w * W + slack for w in range(1, NWIN - 1)] + [total - W]
    first, count = [], []
    for d in range(n_tm):
        meets = [w for w in range(NWIN) if lows[w] < (d + 1) * span and highs[w] + W > d * span]
        assert meets and meets == list(range(meets[0], meets[0] + len(meets)))
        assert len(meets) <= SLOTS
        first.append(meets[0])
        count.append(len(meets))
    return first, count


def _any_of(me, members):
    hit = jnp.bool_(False)
    for m in members:
        hit = hit | (me == m)
    return hit


def _fused_kernel(n_tm, n_chan, bins_dev, first, count,
                  blocks_ref, onehot_ref, mask_ref,
                  white_ref, srcspec_ref,
                  recv, spec, lvl_send, lvl_recv, src_send, src_recv,
                  a2a_send_sem, a2a_recv_sem, lvl_send_sem, lvl_recv_sem,
                  src_send_sem, src_recv_sem):
    me = lax.axis_index("tm")
    mc = lax.axis_index("chan")
    two = [d for d in range(n_tm) if count[d] == 2]
    me_two = _any_of(me, two)

    barrier = pltpu.get_barrier_semaphore()
    for i in range(1, n_tm):
        pl.semaphore_signal(barrier, inc=1, device_id={"tm": lax.rem(me + i, n_tm)},
                            device_id_type=MESH)
    for i in range(1, n_chan):
        pl.semaphore_signal(barrier, inc=1, device_id={"chan": lax.rem(mc + i, n_chan)},
                            device_id_type=MESH)
    pl.semaphore_wait(barrier, n_tm - 1 + n_chan - 1)

    def a2a(peer, slot, src_dev):
        return pltpu.make_async_remote_copy(
            src_ref=blocks_ref.at[peer, slot],
            dst_ref=recv.at[src_dev, slot],
            send_sem=a2a_send_sem.at[peer, slot],
            recv_sem=a2a_recv_sem.at[src_dev, slot],
            device_id={"tm": peer},
            device_id_type=MESH,
        )

    for i in range(1, n_tm):
        peer = lax.rem(me + i, n_tm)
        a2a(peer, 0, me).start()

        @pl.when(me_two)
        def _():
            a2a(peer, 1, me).start()

    recv[me] = blocks_ref[me]
    for i in range(1, n_tm):
        peer = lax.rem(me + i, n_tm)
        a2a(peer, 0, me).wait_send()

        @pl.when(me_two)
        def _():
            a2a(peer, 1, me).wait_send()

    for s in range(n_tm):
        @pl.when(me != s)
        def _():
            a2a(s, 0, s).wait_recv()
            if count[s] == 2:
                a2a(s, 1, s).wait_recv()

    for w in range(NWIN):
        acc = None
        for s in range(n_tm):
            for j in range(count[s]):
                if first[s] + j == w:
                    part = recv[s, j]
                    acc = part if acc is None else acc + part
        spec[w] = acc

    rows = []
    for w in range(NWIN):
        re = spec[w, 0:bins_dev, :]
        im = spec[w, bins_dev:2 * bins_dev, :]
        mag = jnp.sqrt(re * re + im * im)
        rows.append(jnp.sum(mag, axis=0, keepdims=True))
    rows.append(jnp.zeros((8 - NWIN, rows[0].shape[1]), jnp.float32))
    lvl_send[...] = jnp.concatenate(rows, axis=0)

    def lvl(peer, src_dev):
        return pltpu.make_async_remote_copy(
            src_ref=lvl_send,
            dst_ref=lvl_recv.at[src_dev],
            send_sem=lvl_send_sem.at[peer],
            recv_sem=lvl_recv_sem.at[src_dev],
            device_id={"tm": peer},
            device_id_type=MESH,
        )

    for i in range(1, n_tm):
        lvl(lax.rem(me + i, n_tm), me).start()
    lvl_recv[me] = lvl_send[...]
    for i in range(1, n_tm):
        lvl(lax.rem(me + i, n_tm), me).wait_send()
    for i in range(1, n_tm):
        src = lax.rem(me + n_tm - i, n_tm)
        lvl(src, src).wait_recv()

    level = lvl_recv[0]
    for s in range(1, n_tm):
        level = level + lvl_recv[s]
    level = level / F

    mask = mask_ref[...]
    onehot = onehot_ref[...]
    for w in range(NWIN):
        re = spec[w, 0:bins_dev, :]
        im = spec[w, bins_dev:2 * bins_dev, :]
        mag = jnp.sqrt(re * re + im * im)
        den = mag + 0.1 * level[w:w + 1, :] + 1e-06
        for p, part in enumerate((re, im)):
            white = (part / den).astype(jnp.bfloat16).astype(jnp.float32) * mask
            white_ref[2 * w + p] = white
            src_send[2 * w + p] = jnp.dot(
                white.astype(jnp.bfloat16), onehot, preferred_element_type=jnp.float32
            )

    def srcc(peer, src_dev):
        return pltpu.make_async_remote_copy(
            src_ref=src_send,
            dst_ref=src_recv.at[src_dev],
            send_sem=src_send_sem.at[peer],
            recv_sem=src_recv_sem.at[src_dev],
            device_id={"chan": peer},
            device_id_type=MESH,
        )

    for i in range(1, n_chan):
        srcc(lax.rem(mc + i, n_chan), mc).start()
    src_recv[mc] = src_send[...]
    for i in range(1, n_chan):
        srcc(lax.rem(mc + i, n_chan), mc).wait_send()
    for i in range(1, n_chan):
        src = lax.rem(mc + n_chan - i, n_chan)
        srcc(src, src).wait_recv()

    total = src_recv[0]
    for s in range(1, n_chan):
        total = total + src_recv[s]
    srcspec_ref[...] = total


def fused_exchange(blocks, onehot, mask, n_tm, n_chan, bins_dev, first, count):
    channels = blocks.shape[-1]
    nsrc = onehot.shape[1]
    vmem = pl.BlockSpec(memory_space=pltpu.VMEM)
    return pl.pallas_call(
        functools.partial(_fused_kernel, n_tm, n_chan, bins_dev, first, count),
        out_shape=(
            jax.ShapeDtypeStruct((NWIN * 2, bins_dev, channels), jnp.float32),
            jax.ShapeDtypeStruct((NWIN * 2, bins_dev, nsrc), jnp.float32),
        ),
        in_specs=[vmem, vmem, vmem],
        out_specs=(vmem, vmem),
        scratch_shapes=[
            pltpu.VMEM(blocks.shape, jnp.float32),
            pltpu.VMEM((NWIN, 2 * bins_dev, channels), jnp.float32),
            pltpu.VMEM((8, channels), jnp.float32),
            pltpu.VMEM((n_tm, 8, channels), jnp.float32),
            pltpu.VMEM((NWIN * 2, bins_dev, nsrc), jnp.float32),
            pltpu.VMEM((n_chan, NWIN * 2, bins_dev, nsrc), jnp.float32),
            pltpu.SemaphoreType.DMA((n_tm, SLOTS)),
            pltpu.SemaphoreType.DMA((n_tm, SLOTS)),
            pltpu.SemaphoreType.DMA((n_tm,)),
            pltpu.SemaphoreType.DMA((n_tm,)),
            pltpu.SemaphoreType.DMA((n_chan,)),
            pltpu.SemaphoreType.DMA((n_chan,)),
        ],
        compiler_params=pltpu.CompilerParams(collective_id=0, has_side_effects=True),
    )(blocks, onehot, mask)


def phasor(times, bins):
    phase = times[:, None] * bins[None, :] % W
    angle = phase.astype(jnp.float32) * (2.0 * math.pi / W)
    return jnp.cos(angle), -jnp.sin(angle)


def band_basis(times):
    coarse = FLO + FA * jnp.arange(F // FA, dtype=jnp.int32)
    fine = jnp.arange(FA, dtype=jnp.int32)
    ar, ai = phasor(times, coarse)
    br, bi = phasor(times, fine)
    ar, ai = ar[:, :, None], ai[:, :, None]
    br, bi = br[:, None, :], bi[:, None, :]
    re = ar * br - ai * bi
    im = ar * bi + ai * br
    basis = jnp.stack([re, im], axis=-1).reshape(times.shape[0], F, 2)
    return basis.astype(jnp.bfloat16)


def shards(record, offsets, dead_mask, sources):
    n_tm = lax.axis_size("tm")
    n_chan = lax.axis_size("chan")
    bins_dev = F // n_tm
    channels, span = record.shape
    first, count = window_plan(n_tm, span)
    me = lax.axis_index("tm")
    start = me * span
    local_times = start + jnp.arange(span, dtype=jnp.int32)
    wa = jnp.asarray(first, jnp.int32)[me]

    partials = []
    for slot in range(SLOTS):
        window = wa + slot
        origin = offsets[jnp.minimum(window, NWIN - 1)]
        shifted = local_times - origin
        inside = (shifted >= 0) & (shifted < W) & (window < NWIN)
        basis = band_basis(jnp.where(inside, shifted, 0))
        masked = jnp.where(inside[None, :], record, jnp.zeros_like(record))
        part = jnp.einsum("tkp,ct->pkc", basis, masked, preferred_element_type=jnp.float32)
        part = part.reshape(2, n_tm, bins_dev, channels).transpose(1, 0, 2, 3)
        partials.append(part)
    blocks = jnp.stack(partials, axis=1).reshape(n_tm, SLOTS, 2 * bins_dev, channels)

    local_index = sources - lax.axis_index("chan") * channels
    onehot = (jnp.arange(channels, dtype=jnp.int32)[:, None] == local_index[None, :]).astype(
        jnp.bfloat16
    )
    mask = dead_mask.astype(jnp.float32)[None, :]
    white, source_spec = fused_exchange(
        blocks, onehot, mask, n_tm, n_chan, bins_dev, first, count
    )

    left = source_spec.astype(jnp.bfloat16).reshape(NWIN, 2, bins_dev, -1)
    right = white.astype(jnp.bfloat16).reshape(NWIN, 2, bins_dev, channels)
    right_imaginary = jnp.stack([right[:, 1], -right[:, 0]], axis=1)
    real_component = jnp.einsum(
        "wpks,wpkc->ksc", left, right, preferred_element_type=jnp.float32
    )
    imaginary_component = jnp.einsum(
        "wpks,wpkc->ksc", left, right_imaginary, preferred_element_type=jnp.float32
    )
    return jnp.stack([real_component, imaginary_component], axis=1) / NWIN


def solution(mesh):
    return jax.shard_map(
        shards,
        mesh=mesh,
        in_specs=(P("chan", "tm"), P(), P("chan"), P()),
        out_specs=P("tm", None, None, "chan"),
        check_vma=False,
    )
```

time: 112 us -> 122 us (1.089)
  the two profiles are of different devices: /device:TPU:22 before, /device:TPU:118 now
where the time goes in v2:
time: 122 us
  Pallas kernels  78 us (64%)
  local copies, waits for them, and re-layouts  19.3 us (16%)
  other arithmetic  15.6 us (13%)
  matrix products  6.55 us (5%)
  between operations  2.12 us (2%)
    pallas_call x1, Pallas kernels, fused_exchange(): pl.pallas_call(functools.partial(_fused_kernel, n_tm, n_chan, bins_dev, f...  78 us
    sub x2, local copies, waits for them, and re-layouts, band_basis(): re = ar * br - ai * bi  7.92 us
    dot_general x2, matrix products, shards(): jnp.einsum('tkp,ct->pkc', basis, masked, preferred_element_type=jnp.float32)  5.74 us
    another operation x2, other arithmetic  4.72 us
    add x2, local copies, waits for them, and re-layouts, band_basis(): im = ar * bi + ai * br  4.51 us
    cos x3, other arithmetic, phasor(): return (jnp.cos(angle), -jnp.sin(angle))  4.09 us

profile of v2, /device:TPU:118, one launch (start us, length us, event | category | flops | bytes accessed | tf_op | source)
XLA Modules:
  0.0 121.6 jit_solution(13452839286893025608)
XLA Ops:
  0.0 1.2 %dynamic_slice.9 = s32[1]{0:T(128)} dynamic-slice(s32[32]{0:T(128)} %constant.68.clone, s32[]{:T(128)S(6)} %select_n.80), dynamic_slice_sizes={1} | dynamic-slice | bytes 12 | tf_op jit(solution)/shard_map/dynamic_slice | solution.py:236
  2.5 1.3 %fusion.70 = (s32[1]{0:T(128)}, s32[1]{0:T(128)}) fusion(s32[4]{0:T(128)} %param.6, s32[]{:T(128)S(6)} %select_n.81, s32[]{:T(128)S(6)} %select_n.86), kind=kLoop, calls=%fused_computation.92 | loop fusion | bytes 24 | tf_op jit(solution)/shard_map/dynamic_slice | solution.py:241
  4.5 1.2 fusion.54
  5.7 1.6 %fusion.26 = (f32[1536,64]{0,1:T(8,128)S(1)}, f32[1536,64]{0,1:T(8,128)S(1)}) fusion(s32[1536]{0:T(1024)S(1)} %get-tuple-element.27), kind=kLoop, calls=%fused_computation.36 | loop fusion | flops 983040 | bytes 792576 | tf_op jit(solution)/shard_map/cos | solution.py:211
  7.4 0.9 fusion.43
  8.2 2.4 %subtract_convert_fusion.1 = (bf16[1536,10,64]{0,2,1:T(8,128)(2,1)}, bf16[1536,10,64]{0,2,1:T(8,128)(2,1)S(1)}) fusion(f32[1536,64]{0,1:T(8,128)S(1)} %get-tuple-element.20, f32[1536,10]{0,1:T(8,128)S(1)} %get-tuple-element.16, f32[1536,64]{0,1:T(8,128)S(1)} %get-tuple-element.19, f32[1536,10]{0,1:T(8,128)S(1)} %get-tuple-element.15), kind=kLoop, calls=%fused_computation.11 | loop fusion | flops 7864320 | bytes 4841472 | tf_op jit(solution)/shard_map/convert.7
  10.6 4.0 %copy.14 = bf16[1536,640,1]{1,0,2:T(8,128)(2,1)} copy(bf16[1536,640,1]{0,1,2:T(8,128)(2,1)} %bitcast.43) | data formatting | bytes 3932160 | tf_op jit(solution)/shard_map/sub | solution.py:221
  14.6 0.0 copy-start
  14.6 2.3 %copy.15 = bf16[1536,640,1]{1,0,2:T(8,128)(2,1)} copy(bf16[1536,640,1]{0,1,2:T(8,128)(2,1)S(1)} %bitcast.41) | data formatting | bytes 3932160 | tf_op jit(solution)/shard_map/add | solution.py:222
  16.8 1.2 fusion.61
  18.0 0.0 copy-done
  18.0 2.9 %fusion.11 = f32[2,640,128]{1,2,0:T(8,128)S(1)} fusion(bf16[1536,640,1]{1,0,2:T(8,128)(2,1)} %copy.15, bf16[1536,640,1]{1,0,2:T(8,128)(2,1)} %copy.14, bf16[128,1536]{1,0:T(8,128)(2,1)S(1)} %copy-done, pred[1536]{0:T(1024)(128)(4,1)S(1)} %get-tuple-element.30), kind=kOutput, calls=%fused_computation.17 | convolution fusion | flops 511377408 | bytes 4982272 | tf_op jit(solution)/shard_map/tkp,ct->pkc/dot_general | solution.py:246
  20.9 0.8 copy.16
  21.7 0.1 copy.17
  21.8 0.4 copy.22
  22.2 1.6 %fusion.22 = (f32[1536,64]{0,1:T(8,128)S(1)}, f32[1536,64]{0,1:T(8,128)S(1)}) fusion(s32[1536]{0:T(1024)S(1)} %get-tuple-element.28), kind=kLoop, calls=%fused_computation.30 | loop fusion | flops 983040 | bytes 792576 | tf_op jit(solution)/shard_map/cos | solution.py:211
  23.8 2.4 %subtract_convert_fusion = (bf16[1536,10,64]{0,2,1:T(8,128)(2,1)}, bf16[1536,10,64]{0,2,1:T(8,128)(2,1)S(1)}) fusion(f32[1536,64]{0,1:T(8,128)S(1)} %get-tuple-element.22, f32[1536,10]{0,1:T(8,128)S(1)} %get-tuple-element.23, f32[1536,64]{0,1:T(8,128)S(1)} %get-tuple-element.21, f32[1536,10]{0,1:T(8,128)S(1)} %get-tuple-element.24), kind=kLoop, calls=%fused_computation.9 | loop fusion | flops 7864320 | bytes 4841472 | tf_op jit(solution)/shard_map/convert.3
  26.2 4.0 %copy.18 = bf16[1536,640,1]{1,0,2:T(8,128)(2,1)} copy(bf16[1536,640,1]{0,1,2:T(8,128)(2,1)} %bitcast.44) | data formatting | bytes 3932160 | tf_op jit(solution)/shard_map/sub | solution.py:221
  30.1 2.3 %copy.19 = bf16[1536,640,1]{1,0,2:T(8,128)(2,1)} copy(bf16[1536,640,1]{0,1,2:T(8,128)(2,1)S(1)} %bitcast.42) | data formatting | bytes 3932160 | tf_op jit(solution)/shard_map/add | solution.py:222
  32.4 2.9 %fusion.8 = f32[2,640,128]{1,2,0:T(8,128)S(1)} fusion(bf16[1536,640,1]{1,0,2:T(8,128)(2,1)} %copy.19, bf16[1536,640,1]{1,0,2:T(8,128)(2,1)} %copy.18, bf16[128,1536]{1,0:T(8,128)(2,1)S(1)} %copy-done, pred[1536]{0:T(1024)(128)(4,1)S(1)} %get-tuple-element.29), kind=kOutput, calls=%fused_computation.16 | convolution fusion | flops 511377408 | bytes 4982272 | tf_op jit(solution)/shard_map/tkp,ct->pkc/dot_general | solution.py:246
  35.3 0.8 copy.20
  36.0 0.0 copy-start.1
  36.0 0.0 copy-start.2
  36.1 0.1 copy.21
  36.2 0.4 copy.23
  36.6 1.1 pad_maximum_fusion.blocks_ref
  37.7 0.0 copy-done.1
  37.7 0.6 fusion.46.onehot_ref
  38.4 0.0 copy-done.2
  38.4 0.5 convert_bitcast_fusion.mask_ref
  38.9 78.0 %shard_map.55 = (f32[8,20,128]{2,1,0:T(8,128)}, f32[8,20,128]{2,1,0:T(8,128)}) custom-call(f32[32,2,40,128]{3,2,1,0:T(8,128)} %pad_maximum_fusion.blocks_ref, bf16[128,128]{1,0:T(8,128)(2,1)} %fusion.46.onehot_ref, f32[1,128]{1,0:T(1,128)} %convert_bitcast_fusion.mask_ref), custom_call_target="tpu_custom_call" | custom-call | tf_op jit(solution)/shard_map/pallas_call | solution.py:182
  116.9 0.9 convert_element_type.61
  117.9 0.9 convert_element_type.60
  118.8 0.4 convolution_bitcast_fusion.1
  119.2 0.4 convolution_bitcast_fusion
  119.6 0.3 maximum_multiply_fusion
  119.9 1.7 %copy.29 = f32[20,2,128,128]{3,2,1,0:T(8,128)} copy(f32[20,2,128,128]{3,2,0,1:T(8,128)S(1)} %maximum_multiply_fusion) | data formatting | bytes 5242880 | tf_op jit(solution)/shard_map/div | solution.py:269
  (4 shorter events, 0.0 us)
Async XLA Ops:
  14.6 3.5 %copy-start = (bf16[128,1536]{1,0:T(8,128)(2,1)S(1)}, bf16[128,1536]{1,0:T(8,128)(2,1)}, u32[]{:S(2)}) copy-start(bf16[128,1536]{1,0:T(8,128)(2,1)} %param.5) | copy-start | bytes 1179652
  36.0 1.7 %copy-start.1 = (s32[128]{0:T(128)S(1)}, s32[128]{0:T(128)}, u32[]{:S(2)}) copy-start(s32[128]{0:T(128)} %param.8) | copy-start | bytes 1540
  36.0 2.3 %copy-start.2 = (s32[128]{0:T(128)S(1)}, s32[128]{0:T(128)}, u32[]{:S(2)}) copy-start(s32[128]{0:T(128)} %param.7) | copy-start | bytes 1540

commit v3 on v2

--- a/solution.py
+++ b/solution.py
@@ -105,8 +105,8 @@
 
     rows = []
     for w in range(NWIN):
-        re = spec[w, 0:bins_dev, :]
-        im = spec[w, bins_dev:2 * bins_dev, :]
+        re = spec[w, pl.ds(0, bins_dev, stride=2), :]
+        im = spec[w, pl.ds(1, bins_dev, stride=2), :]
         mag = jnp.sqrt(re * re + im * im)
         rows.append(jnp.sum(mag, axis=0, keepdims=True))
     rows.append(jnp.zeros((8 - NWIN, rows[0].shape[1]), jnp.float32))
@@ -139,8 +139,8 @@
     mask = mask_ref[...]
     onehot = onehot_ref[...]
     for w in range(NWIN):
-        re = spec[w, 0:bins_dev, :]
-        im = spec[w, bins_dev:2 * bins_dev, :]
+        re = spec[w, pl.ds(0, bins_dev, stride=2), :]
+        im = spec[w, pl.ds(1, bins_dev, stride=2), :]
         mag = jnp.sqrt(re * re + im * im)
         den = mag + 0.1 * level[w:w + 1, :] + 1e-06
         for p, part in enumerate((re, im)):
@@ -243,9 +243,8 @@
         inside = (shifted >= 0) & (shifted < W) & (window < NWIN)
         basis = band_basis(jnp.where(inside, shifted, 0))
         masked = jnp.where(inside[None, :], record, jnp.zeros_like(record))
-        part = jnp.einsum("tkp,ct->pkc", basis, masked, preferred_element_type=jnp.float32)
-        part = part.reshape(2, n_tm, bins_dev, channels).transpose(1, 0, 2, 3)
-        partials.append(part)
+        part = jnp.einsum("tkp,ct->kpc", basis, masked, preferred_element_type=jnp.float32)
+        partials.append(part.reshape(n_tm, 2 * bins_dev, channels))
     blocks = jnp.stack(partials, axis=1).reshape(n_tm, SLOTS, 2 * bins_dev, channels)
 
     local_index = sources - lax.axis_index("chan") * channels

time: 122 us -> 136 us (1.11)
  local copies, waits for them, and re-layouts: 19.3 us -> 34.3 us
  other arithmetic: 15.6 us -> 13.9 us
    another operation x2, local copies, waits for them, and re-layouts: 0.77 us -> 18.1 us  [shards(): jnp.stack(partials, axis=1).reshape(n_tm, SLOTS, 2 * bins_dev, channels)]
    dot_general x0 -> x2, local copies, waits for them, and re-layouts: none -> 11.8 us  [shards(): jnp.einsum('tkp,ct->kpc', basis, masked, preferred_element_type=jnp.float32)]
    sub x2 -> x0, local copies, waits for them, and re-layouts: 7.92 us -> none  [band_basis(): re = ar * br - ai * bi]
    add x2 -> x0, local copies, waits for them, and re-layouts: 4.51 us -> none  [band_basis(): im = ar * bi + ai * br]
    another operation x2, other arithmetic: 4.72 us -> 2.11 us
    transpose x4 -> x0, local copies, waits for them, and re-layouts: 1.79 us -> none  [the longest x2 1.53 us: shards(): jnp.einsum('tkp,ct->pkc', basis, masked, preferred_element_type=jnp.float32)]
where the time goes in v3:
time: 136 us
  Pallas kernels  78 us (57%)
  local copies, waits for them, and re-layouts  34.3 us (25%)
  other arithmetic  13.9 us (10%)
  matrix products  7.53 us (6%)
  between operations  2.09 us (2%)
    pallas_call x1, Pallas kernels, fused_exchange(): pl.pallas_call(functools.partial(_fused_kernel, n_tm, n_chan, bins_dev, f...  78 us
    another operation x2, local copies, waits for them, and re-layouts  18.1 us
    dot_general x2, local copies, waits for them, and re-layouts, shards(): jnp.einsum('tkp,ct->kpc', basis, masked, preferred_element_type=jnp.float32)  11.8 us
    dot_general x2, matrix products, shards(): jnp.einsum('tkp,ct->kpc', basis, masked, preferred_element_type=jnp.float32)  6.71 us
    cos x3, other arithmetic, phasor(): return (jnp.cos(angle), -jnp.sin(angle))  4.09 us

profile of v3, /device:TPU:118, one launch (start us, length us, event | category | flops | bytes accessed | tf_op | source)
XLA Modules:
  0.0 135.8 jit_solution(1640345298211149362)
XLA Ops:
  0.0 1.2 dynamic_slice.9
  2.5 1.4 %fusion.54 = (s32[1]{0:T(128)}, s32[1]{0:T(128)}) fusion(s32[4]{0:T(128)} %param.6, s32[]{:T(128)S(6)} %select_n.81, s32[]{:T(128)S(6)} %select_n.86), kind=kLoop, calls=%fused_computation.84 | loop fusion | bytes 24 | tf_op jit(solution)/shard_map/dynamic_slice | solution.py:241
  4.6 1.3 fusion.40
  5.9 1.6 %fusion.13 = (f32[1536,64]{0,1:T(8,128)S(1)}, f32[1536,64]{0,1:T(8,128)S(1)}) fusion(s32[1536]{0:T(1024)S(1)} %get-tuple-element.27), kind=kLoop, calls=%fused_computation.31 | loop fusion | flops 983040 | bytes 792576 | tf_op jit(solution)/shard_map/cos | solution.py:211
  7.5 0.9 fusion.29
  8.4 1.1 subtract_convert_fusion.1
  9.5 0.4 maximum_bitcast_fusion
  9.8 5.9 %copy.12 = bf16[640,2,1536]{2,1,0:T(2,128)(2,1)} copy(bf16[640,2,1536]{2,0,1:T(8,128)(2,1)S(1)} %maximum_bitcast_fusion) | data formatting | bytes 7864320 | tf_op jit(solution)/shard_map/tkp,ct->kpc/dot_general | solution.py:246
  15.7 0.0 copy-start
  15.7 9.1 %reshape.484 = bf16[32,40,1536]{2,1,0:T(8,128)(2,1)} reshape(bf16[640,2,1536]{2,1,0:T(2,128)(2,1)} %copy.12) | data formatting | bytes 7864320 | tf_op jit(solution)/shard_map/reshape.103
  24.8 1.3 fusion.47
  26.1 0.0 copy-done
  26.1 3.3 %convolution_bitcast_fusion.3 = f32[32,1,40,128]{3,2,1,0:T(8,128)S(1)} fusion(bf16[32,40,1536]{2,1,0:T(8,128)(2,1)} %reshape.484, bf16[128,1536]{1,0:T(8,128)(2,1)S(1)} %copy-done, pred[1536]{0:T(1024)(128)(4,1)S(1)} %get-tuple-element.30), kind=kOutput, calls=%fused_computation.11 | convolution fusion | flops 503513088 | bytes 4982272 | tf_op jit(solution)/shard_map/tkp,ct->kpc/dot_general | solution.py:246
  29.4 1.6 %fusion.9 = (f32[1536,64]{0,1:T(8,128)S(1)}, f32[1536,64]{0,1:T(8,128)S(1)}) fusion(s32[1536]{0:T(1024)S(1)} %get-tuple-element.28), kind=kLoop, calls=%fused_computation.25 | loop fusion | flops 983040 | bytes 792576 | tf_op jit(solution)/shard_map/cos | solution.py:211
  31.1 1.0 subtract_convert_fusion
  32.1 0.4 maximum_bitcast_fusion.1
  32.5 5.9 %copy.13 = bf16[640,2,1536]{2,1,0:T(2,128)(2,1)} copy(bf16[640,2,1536]{2,0,1:T(8,128)(2,1)S(1)} %maximum_bitcast_fusion.1) | data formatting | bytes 7864320 | tf_op jit(solution)/shard_map/tkp,ct->kpc/dot_general | solution.py:246
  38.4 9.0 %reshape.485 = bf16[32,40,1536]{2,1,0:T(8,128)(2,1)} reshape(bf16[640,2,1536]{2,1,0:T(2,128)(2,1)} %copy.13) | data formatting | bytes 7864320 | tf_op jit(solution)/shard_map/reshape.129
  47.4 0.0 copy-start.1
  47.4 0.0 copy-start.2
  47.4 3.4 %convolution_bitcast_fusion.2 = f32[32,1,40,128]{3,2,1,0:T(8,128)S(1)} fusion(bf16[32,40,1536]{2,1,0:T(8,128)(2,1)} %reshape.485, bf16[128,1536]{1,0:T(8,128)(2,1)S(1)} %copy-done, pred[1536]{0:T(1024)(128)(4,1)S(1)} %get-tuple-element.29), kind=kOutput, calls=%fused_computation.10 | convolution fusion | flops 503513088 | bytes 4982272 | tf_op jit(solution)/shard_map/tkp,ct->kpc/dot_general | solution.py:246
  50.8 1.1 pad_maximum_fusion.blocks_ref
  51.9 0.0 copy-done.1
  51.9 0.6 fusion.32.onehot_ref
  52.6 0.0 copy-done.2
  52.6 0.5 convert_bitcast_fusion.mask_ref
  53.1 78.0 %shard_map.55 = (f32[8,20,128]{2,1,0:T(8,128)}, f32[8,20,128]{2,1,0:T(8,128)}) custom-call(f32[32,2,40,128]{3,2,1,0:T(8,128)} %pad_maximum_fusion.blocks_ref, bf16[128,128]{1,0:T(8,128)(2,1)} %fusion.32.onehot_ref, f32[1,128]{1,0:T(1,128)} %convert_bitcast_fusion.mask_ref), custom_call_target="tpu_custom_call" | custom-call | tf_op jit(solution)/shard_map/pallas_call | solution.py:182
  131.1 0.9 convert_element_type.61
  132.1 0.9 convert_element_type.60
  133.0 0.4 convolution_bitcast_fusion.1
  133.4 0.4 convolution_bitcast_fusion
  133.8 0.3 maximum_multiply_fusion
  134.1 1.7 %copy.19 = f32[20,2,128,128]{3,2,1,0:T(8,128)} copy(f32[20,2,128,128]{3,2,0,1:T(8,128)S(1)} %maximum_multiply_fusion) | data formatting | bytes 5242880 | tf_op jit(solution)/shard_map/div | solution.py:268
  (4 shorter events, 0.0 us)
Async XLA Ops:
  15.7 10.4 %copy-start = (bf16[128,1536]{1,0:T(8,128)(2,1)S(1)}, bf16[128,1536]{1,0:T(8,128)(2,1)}, u32[]{:S(2)}) copy-start(bf16[128,1536]{1,0:T(8,128)(2,1)} %param.5) | copy-start | bytes 1179652
  47.4 4.5 %copy-start.1 = (s32[128]{0:T(128)S(1)}, s32[128]{0:T(128)}, u32[]{:S(2)}) copy-start(s32[128]{0:T(128)} %param.8) | copy-start | bytes 1540
  47.4 5.2 %copy-start.2 = (s32[128]{0:T(128)S(1)}, s32[128]{0:T(128)}, u32[]{:S(2)}) copy-start(s32[128]{0:T(128)} %param.7) | copy-start | bytes 1540

commit v4 on v2

--- a/solution.py
+++ b/solution.py
@@ -205,23 +205,42 @@
     )(blocks, onehot, mask)
 
 
-def phasor(times, bins):
-    phase = times[:, None] * bins[None, :] % W
+def _dft_kernel(n_tm, bins_dev, ar_ref, ai_ref, c1_ref, c2_ref, x_ref, o_ref, lhs):
+    group = lhs.shape[0] // (2 * bins_dev)
+    for slot in range(SLOTS):
+        c1 = c1_ref[slot]
+        c2 = c2_ref[slot]
+        x = x_ref[slot]
+        for g in range(n_tm // group):
+            for dd in range(group):
+                d = g * group + dd
+                ar = ar_ref[slot, d:d + 1, :]
+                ai = ai_ref[slot, d:d + 1, :]
+                lhs[dd * 2 * bins_dev:(dd + 1) * 2 * bins_dev, :] = ar * c1 + ai * c2
+            res = lax.dot_general(
+                lhs[...].astype(jnp.bfloat16), x, (((1,), (1,)), ((), ())),
+                preferred_element_type=jnp.float32,
+            )
+            o_ref[g * group:(g + 1) * group, slot] = res.reshape(group, 2 * bins_dev, x.shape[0])
+
+
+def dft(ar, ai, c1, c2, x, n_tm, bins_dev):
+    channels, span = x.shape[1], x.shape[2]
+    group = 8
+    vmem = pl.BlockSpec(memory_space=pltpu.VMEM)
+    return pl.pallas_call(
+        functools.partial(_dft_kernel, n_tm, bins_dev),
+        out_shape=jax.ShapeDtypeStruct((n_tm, SLOTS, 2 * bins_dev, channels), jnp.float32),
+        in_specs=[vmem] * 5,
+        out_specs=vmem,
+        scratch_shapes=[pltpu.VMEM((group * 2 * bins_dev, span), jnp.float32)],
+    )(ar, ai, c1, c2, x)
+
+
+def phasor(bins, times):
+    phase = bins[:, None] * times[None, :] % W
     angle = phase.astype(jnp.float32) * (2.0 * math.pi / W)
     return jnp.cos(angle), -jnp.sin(angle)
-
-
-def band_basis(times):
-    coarse = FLO + FA * jnp.arange(F // FA, dtype=jnp.int32)
-    fine = jnp.arange(FA, dtype=jnp.int32)
-    ar, ai = phasor(times, coarse)
-    br, bi = phasor(times, fine)
-    ar, ai = ar[:, :, None], ai[:, :, None]
-    br, bi = br[:, None, :], bi[:, None, :]
-    re = ar * br - ai * bi
-    im = ar * bi + ai * br
-    basis = jnp.stack([re, im], axis=-1).reshape(times.shape[0], F, 2)
-    return basis.astype(jnp.bfloat16)
 
 
 def shards(record, offsets, dead_mask, sources):
@@ -234,19 +253,25 @@
     start = me * span
     local_times = start + jnp.arange(span, dtype=jnp.int32)
     wa = jnp.asarray(first, jnp.int32)[me]
-
-    partials = []
+    coarse = FLO + bins_dev * jnp.arange(n_tm, dtype=jnp.int32)
+    fine = jnp.arange(bins_dev, dtype=jnp.int32)
+
+    ars, ais, c1s, c2s, xs = [], [], [], [], []
     for slot in range(SLOTS):
         window = wa + slot
         origin = offsets[jnp.minimum(window, NWIN - 1)]
         shifted = local_times - origin
         inside = (shifted >= 0) & (shifted < W) & (window < NWIN)
-        basis = band_basis(jnp.where(inside, shifted, 0))
-        masked = jnp.where(inside[None, :], record, jnp.zeros_like(record))
-        part = jnp.einsum("tkp,ct->pkc", basis, masked, preferred_element_type=jnp.float32)
-        part = part.reshape(2, n_tm, bins_dev, channels).transpose(1, 0, 2, 3)
-        partials.append(part)
-    blocks = jnp.stack(partials, axis=1).reshape(n_tm, SLOTS, 2 * bins_dev, channels)
+        times = jnp.where(inside, shifted, 0)
+        ar, ai = phasor(coarse, times)
+        br, bi = phasor(fine, times)
+        ars.append(ar)
+        ais.append(ai)
+        c1s.append(jnp.concatenate([br, bi], axis=0))
+        c2s.append(jnp.concatenate([-bi, br], axis=0))
+        xs.append(jnp.where(inside[None, :], record, jnp.zeros_like(record)))
+    blocks = dft(jnp.stack(ars), jnp.stack(ais), jnp.stack(c1s), jnp.stack(c2s),
+                 jnp.stack(xs), n_tm, bins_dev)
 
     local_index = sources - lax.axis_index("chan") * channels
     onehot = (jnp.arange(channels, dtype=jnp.int32)[:, None] == local_index[None, :]).astype(

time: 122 us -> 105 us (0.86)
  local copies, waits for them, and re-layouts: 19.3 us -> 4.28 us
  matrix products: 6.55 us -> 0.81 us
  Pallas kernels: 78 us -> 83.1 us
    sub x2 -> x0, local copies, waits for them, and re-layouts: 7.92 us -> none  [band_basis(): re = ar * br - ai * bi]
    dot_general x2 -> x0, matrix products: 5.74 us -> none  [shards(): jnp.einsum('tkp,ct->pkc', basis, masked, preferred_element_type=jnp.float32)]
    pallas_call x0 -> x1, Pallas kernels: none -> 5.05 us  [dft(): pl.pallas_call(functools.partial(_dft_kernel, n_tm, bins_dev), out_shape=...]
    add x2 -> x0, local copies, waits for them, and re-layouts: 4.51 us -> none  [band_basis(): im = ar * bi + ai * br]
    cos x3 -> x0, other arithmetic: 4.09 us -> none  [phasor(): return (jnp.cos(angle), -jnp.sin(angle))]
    transpose x4 -> x0, local copies, waits for them, and re-layouts: 1.79 us -> none  [the longest x2 1.53 us: shards(): jnp.einsum('tkp,ct->pkc', basis, masked, preferred_element_type=jnp.float32)]
    neg x0 -> x1, other arithmetic: none -> 1.66 us  [phasor(): return (jnp.cos(angle), -jnp.sin(angle))]
    another operation x3 -> x8, other arithmetic: 5.87 us -> 4.32 us  [the longest x2 1.02 us: shards(): jnp.stack(xs)]
where the time goes in v4:
time: 105 us
  Pallas kernels  83.1 us (79%)
  other arithmetic  14.4 us (14%)
  local copies, waits for them, and re-layouts  4.28 us (4%)
  between operations  2.06 us (2%)
    pallas_call x1, Pallas kernels, fused_exchange(): pl.pallas_call(functools.partial(_fused_kernel, n_tm, n_chan, bins_dev, f...  78 us
    pallas_call x1, Pallas kernels, dft(): pl.pallas_call(functools.partial(_dft_kernel, n_tm, bins_dev), out_shape=...  5.05 us

profile of v4, /device:TPU:118, one launch (start us, length us, event | category | flops | bytes accessed | tf_op | source)
XLA Modules:
  0.0 104.7 jit_solution(6636891406691530636)
XLA Ops:
  0.0 0.7 broadcast_subtract_fusion
  0.7 1.2 %dynamic_slice.9 = s32[1]{0:T(128)} dynamic-slice(s32[32]{0:T(128)} %constant.68.clone, s32[]{:T(128)S(6)} %select_n.74), dynamic_slice_sizes={1} | dynamic-slice | bytes 12 | tf_op jit(solution)/shard_map/dynamic_slice | solution.py:255
  3.9 1.3 %fusion.48 = (s32[1]{0:T(128)}, s32[1]{0:T(128)}) fusion(s32[4]{0:T(128)} %param.6, s32[]{:T(128)S(6)} %select_n.75, s32[]{:T(128)S(6)} %select_n.78), kind=kLoop, calls=%fused_computation.78 | loop fusion | bytes 24 | tf_op jit(solution)/shard_map/dynamic_slice | solution.py:262
  5.2 1.2 %convert_bitcast_fusion.mask_ref = f32[1,128]{1,0:T(1,128)} fusion(s32[128]{0:T(128)} %param.7), kind=kLoop, calls=%fused_computation.73 | loop fusion | flops 128 | bytes 1024 | tf_op jit(solution)/shard_map/broadcast_in_dim | solution.py:280
  6.5 1.3 %fusion.43 = (pred[1536]{0:T(1024)(128)(4,1)S(1)}, pred[1536]{0:T(1024)(128)(4,1)S(1)}) fusion(s32[]{:T(128)} %bitcast.4, s32[]{:T(128)S(6)} %mul.129, pred[]{:T(512)} %bitcast.5, pred[]{:T(512)} %bitcast.2, s32[]{:T(128)} %bitcast.1), kind=kLoop, calls=%fused_computation.70 | loop fusion | flops 16896 | bytes 3086 | tf_op jit(solution)/shard_map/and | solution.py:264
  7.8 1.3 %fusion.36 = (s32[1536]{0:T(1024)S(1)}, s32[1536]{0:T(1024)S(1)}) fusion(s32[]{:T(128)} %bitcast.1, s32[]{:T(128)S(6)} %mul.129, pred[]{:T(512)} %bitcast.2, pred[]{:T(512)} %bitcast.5, s32[]{:T(128)} %bitcast.4), kind=kLoop, calls=%fused_computation.63 | loop fusion | flops 19968 | bytes 12302 | tf_op jit(solution)/shard_map/jit(_where)/select_n | solution.py:265
  9.1 0.6 fusion.26.onehot_ref
  9.7 0.6 fusion.22
  10.3 0.6 fusion.18
  10.9 0.0 copy-start
  11.0 0.8 pad_maximum_fusion.2.c2_ref
  11.8 0.8 pad_maximum_fusion.1.c1_ref
  12.7 1.7 %sine_negate_fusion.1 = (f32[1,32,1536]{2,1,0:T(8,128)S(1)}, f32[1,32,1536]{2,1,0:T(8,128)S(1)}, f32[1,32,1536]{2,1,0:T(8,128)S(1)}, f32[1,32,1536]{2,1,0:T(8,128)S(1)}) fusion(s32[1536]{0:T(1024)S(1)} %get-tuple-element.31, s32[32]{0:T(128)S(1)} %multiply_add_fusion, s32[1536]{0:T(1024)S(1)} %get-tuple-element.32), kind=kLoop, calls=%fused_computation.23 | loop fusion | flops 983040 | bytes 798848 | tf_op jit(solution)/shard_map/neg | solution.py:243
  14.3 0.8 pad_maximum_fusion.4.ai_ref
  15.1 0.8 pad_maximum_fusion.3.ar_ref
  15.9 0.0 copy-done
  15.9 0.1 select_bitcast_fusion.1
  16.0 1.0 pad_maximum_fusion.x_ref
  16.9 5.0 %shard_map.55.blocks_ref = f32[32,2,40,128]{3,2,1,0:T(8,128)} custom-call(f32[2,32,1536]{2,1,0:T(8,128)} %pad_maximum_fusion.3.ar_ref, f32[2,32,1536]{2,1,0:T(8,128)} %pad_maximum_fusion.4.ai_ref, f32[2,40,1536]{2,1,0:T(8,128)} %pad_maximum_fusion.1.c1_ref, f32[2,40,1536]{2,1,0:T(8,128)} %pad_maximum_fusion.2.c2_ref, bf16[2,128,1536]{2,1,0:T(8,128)(2,1)} %pad_maximum_fusion.x_ref), custom_call_target="tpu_custom_call" | custom-call | tf_op jit(solution)/shard_map/pallas_call | solution.py:231
  22.0 78.0 %shard_map.56 = (f32[8,20,128]{2,1,0:T(8,128)}, f32[8,20,128]{2,1,0:T(8,128)}) custom-call(f32[32,2,40,128]{3,2,1,0:T(8,128)} %shard_map.55.blocks_ref, bf16[128,128]{1,0:T(8,128)(2,1)} %fusion.26.onehot_ref, f32[1,128]{1,0:T(1,128)} %convert_bitcast_fusion.mask_ref), custom_call_target="tpu_custom_call" | custom-call | tf_op jit(solution)/shard_map/pallas_call | solution.py:182
  100.0 0.9 convert_element_type.52
  100.9 0.9 convert_element_type.53
  101.9 0.4 convolution_bitcast_fusion
  102.3 0.4 convolution_bitcast_fusion.1
  102.7 0.3 maximum_multiply_fusion
  103.0 1.7 %copy.11 = f32[20,2,128,128]{3,2,1,0:T(8,128)} copy(f32[20,2,128,128]{3,2,0,1:T(8,128)S(1)} %maximum_multiply_fusion) | data formatting | bytes 5242880 | tf_op jit(solution)/shard_map/div | solution.py:294
  (5 shorter events, 0.1 us)
Async XLA Ops:
  10.9 4.9 %copy-start = (bf16[128,1536]{1,0:T(8,128)(2,1)S(1)}, bf16[128,1536]{1,0:T(8,128)(2,1)}, u32[]{:S(2)}) copy-start(bf16[128,1536]{1,0:T(8,128)(2,1)} %param.5) | copy-start | bytes 1179652

commit v5 on v4

--- a/solution.py
+++ b/solution.py
@@ -41,15 +41,17 @@
 
 
 def _fused_kernel(n_tm, n_chan, bins_dev, first, count,
-                  blocks_ref, onehot_ref, mask_ref,
+                  ar_ref, ai_ref, c1_ref, c2_ref, x_ref, onehot_ref, mask_ref,
                   white_ref, srcspec_ref,
-                  recv, spec, lvl_send, lvl_recv, src_send, src_recv,
+                  blocks_ref, lhs, recv, spec, lvl_send, lvl_recv, src_send, src_recv,
                   a2a_send_sem, a2a_recv_sem, lvl_send_sem, lvl_recv_sem,
                   src_send_sem, src_recv_sem):
     me = lax.axis_index("tm")
     mc = lax.axis_index("chan")
     two = [d for d in range(n_tm) if count[d] == 2]
     me_two = _any_of(me, two)
+    rows = 2 * bins_dev
+    group = lhs.shape[0] // rows
 
     barrier = pltpu.get_barrier_semaphore()
     for i in range(1, n_tm):
@@ -58,7 +60,6 @@
     for i in range(1, n_chan):
         pl.semaphore_signal(barrier, inc=1, device_id={"chan": lax.rem(mc + i, n_chan)},
                             device_id_type=MESH)
-    pl.semaphore_wait(barrier, n_tm - 1 + n_chan - 1)
 
     def a2a(peer, slot, src_dev):
         return pltpu.make_async_remote_copy(
@@ -70,15 +71,45 @@
             device_id_type=MESH,
         )
 
-    for i in range(1, n_tm):
-        peer = lax.rem(me + i, n_tm)
-        a2a(peer, 0, me).start()
+    def compute(g, slot):
+        c1 = c1_ref[slot]
+        c2 = c2_ref[slot]
+        for dd in range(group):
+            d = lax.rem(me + g * group + dd, n_tm)
+            ar = ar_ref[slot, pl.ds(d, 1), :]
+            ai = ai_ref[slot, pl.ds(d, 1), :]
+            lhs[dd * rows:(dd + 1) * rows, :] = ar * c1 + ai * c2
+        res = lax.dot_general(
+            lhs[...].astype(jnp.bfloat16), x_ref[slot], (((1,), (1,)), ((), ())),
+            preferred_element_type=jnp.float32,
+        )
+        for dd in range(group):
+            d = lax.rem(me + g * group + dd, n_tm)
+            blocks_ref[d, slot] = res[dd * rows:(dd + 1) * rows, :]
+
+    def send(g, slot):
+        for dd in range(group):
+            if g == 0 and dd == 0:
+                continue
+            a2a(lax.rem(me + g * group + dd, n_tm), slot, me).start()
+
+    for g in range(n_tm // group):
+        compute(g, 0)
+        if g == 0:
+            pl.semaphore_wait(barrier, n_tm - 1 + n_chan - 1)
+        send(g, 0)
 
         @pl.when(me_two)
         def _():
-            a2a(peer, 1, me).start()
-
-    recv[me] = blocks_ref[me]
+            compute(g, 1)
+            send(g, 1)
+
+    recv[me, 0] = blocks_ref[me, 0]
+
+    @pl.when(me_two)
+    def _():
+        recv[me, 1] = blocks_ref[me, 1]
+
     for i in range(1, n_tm):
         peer = lax.rem(me + i, n_tm)
         a2a(peer, 0, me).wait_send()
@@ -175,9 +206,10 @@
     srcspec_ref[...] = total
 
 
-def fused_exchange(blocks, onehot, mask, n_tm, n_chan, bins_dev, first, count):
-    channels = blocks.shape[-1]
+def fused_exchange(ar, ai, c1, c2, x, onehot, mask, n_tm, n_chan, bins_dev, first, count):
+    channels, span = x.shape[1], x.shape[2]
     nsrc = onehot.shape[1]
+    group = 8
     vmem = pl.BlockSpec(memory_space=pltpu.VMEM)
     return pl.pallas_call(
         functools.partial(_fused_kernel, n_tm, n_chan, bins_dev, first, count),
@@ -185,10 +217,12 @@
             jax.ShapeDtypeStruct((NWIN * 2, bins_dev, channels), jnp.float32),
             jax.ShapeDtypeStruct((NWIN * 2, bins_dev, nsrc), jnp.float32),
         ),
-        in_specs=[vmem, vmem, vmem],
+        in_specs=[vmem] * 7,
         out_specs=(vmem, vmem),
         scratch_shapes=[
-            pltpu.VMEM(blocks.shape, jnp.float32),
+            pltpu.VMEM((n_tm, SLOTS, 2 * bins_dev, channels), jnp.float32),
+            pltpu.VMEM((group * 2 * bins_dev, span), jnp.float32),
+            pltpu.VMEM((n_tm, SLOTS, 2 * bins_dev, channels), jnp.float32),
             pltpu.VMEM((NWIN, 2 * bins_dev, channels), jnp.float32),
             pltpu.VMEM((8, channels), jnp.float32),
             pltpu.VMEM((n_tm, 8, channels), jnp.float32),
@@ -202,39 +236,7 @@
             pltpu.SemaphoreType.DMA((n_chan,)),
         ],
         compiler_params=pltpu.CompilerParams(collective_id=0, has_side_effects=True),
-    )(blocks, onehot, mask)
-
-
-def _dft_kernel(n_tm, bins_dev, ar_ref, ai_ref, c1_ref, c2_ref, x_ref, o_ref, lhs):
-    group = lhs.shape[0] // (2 * bins_dev)
-    for slot in range(SLOTS):
-        c1 = c1_ref[slot]
-        c2 = c2_ref[slot]
-        x = x_ref[slot]
-        for g in range(n_tm // group):
-            for dd in range(group):
-                d = g * group + dd
-                ar = ar_ref[slot, d:d + 1, :]
-                ai = ai_ref[slot, d:d + 1, :]
-                lhs[dd * 2 * bins_dev:(dd + 1) * 2 * bins_dev, :] = ar * c1 + ai * c2
-            res = lax.dot_general(
-                lhs[...].astype(jnp.bfloat16), x, (((1,), (1,)), ((), ())),
-                preferred_element_type=jnp.float32,
-            )
-            o_ref[g * group:(g + 1) * group, slot] = res.reshape(group, 2 * bins_dev, x.shape[0])
-
-
-def dft(ar, ai, c1, c2, x, n_tm, bins_dev):
-    channels, span = x.shape[1], x.shape[2]
-    group = 8
-    vmem = pl.BlockSpec(memory_space=pltpu.VMEM)
-    return pl.pallas_call(
-        functools.partial(_dft_kernel, n_tm, bins_dev),
-        out_shape=jax.ShapeDtypeStruct((n_tm, SLOTS, 2 * bins_dev, channels), jnp.float32),
-        in_specs=[vmem] * 5,
-        out_specs=vmem,
-        scratch_shapes=[pltpu.VMEM((group * 2 * bins_dev, span), jnp.float32)],
-    )(ar, ai, c1, c2, x)
+    )(ar, ai, c1, c2, x, onehot, mask)
 
 
 def phasor(bins, times):
@@ -270,8 +272,6 @@
         c1s.append(jnp.concatenate([br, bi], axis=0))
         c2s.append(jnp.concatenate([-bi, br], axis=0))
         xs.append(jnp.where(inside[None, :], record, jnp.zeros_like(record)))
-    blocks = dft(jnp.stack(ars), jnp.stack(ais), jnp.stack(c1s), jnp.stack(c2s),
-                 jnp.stack(xs), n_tm, bins_dev)
 
     local_index = sources - lax.axis_index("chan") * channels
     onehot = (jnp.arange(channels, dtype=jnp.int32)[:, None] == local_index[None, :]).astype(
@@ -279,7 +279,8 @@
     )
     mask = dead_mask.astype(jnp.float32)[None, :]
     white, source_spec = fused_exchange(
-        blocks, onehot, mask, n_tm, n_chan, bins_dev, first, count
+        jnp.stack(ars), jnp.stack(ais), jnp.stack(c1s), jnp.stack(c2s), jnp.stack(xs),
+        onehot, mask, n_tm, n_chan, bins_dev, first, count
     )
 
     left = source_spec.astype(jnp.bfloat16).reshape(NWIN, 2, bins_dev, -1)

time: 105 us -> 101 us (0.962)
  the two profiles are of different devices: /device:TPU:118 before, /device:TPU:166 now
where the time goes in v5:
time: 101 us
  Pallas kernels  79.1 us (78%)
  other arithmetic  14.3 us (14%)
  local copies, waits for them, and re-layouts  4.28 us (4%)
  between operations  2.06 us (2%)
    pallas_call x1, Pallas kernels, fused_exchange(): pl.pallas_call(functools.partial(_fused_kernel, n_tm, n_chan, bins_dev, f...  79.1 us

profile of v5, /device:TPU:166, one launch (start us, length us, event | category | flops | bytes accessed | tf_op | source)
XLA Modules:
  0.0 100.6 jit_solution(14505665213407525740)
XLA Ops:
  0.0 0.7 broadcast_subtract_fusion
  0.7 1.2 %dynamic_slice.9 = s32[1]{0:T(128)} dynamic-slice(s32[32]{0:T(128)} %constant.68.clone, s32[]{:T(128)S(6)} %select_n.74), dynamic_slice_sizes={1} | dynamic-slice | bytes 12 | tf_op jit(solution)/shard_map/dynamic_slice | solution.py:257
  3.9 1.3 %fusion.48 = (s32[1]{0:T(128)}, s32[1]{0:T(128)}) fusion(s32[4]{0:T(128)} %param.6, s32[]{:T(128)S(6)} %select_n.75, s32[]{:T(128)S(6)} %select_n.78), kind=kLoop, calls=%fused_computation.78 | loop fusion | bytes 24 | tf_op jit(solution)/shard_map/dynamic_slice | solution.py:264
  5.2 1.2 %convert_bitcast_fusion.mask_ref = f32[1,128]{1,0:T(1,128)} fusion(s32[128]{0:T(128)} %param.7), kind=kLoop, calls=%fused_computation.73 | loop fusion | flops 128 | bytes 1024 | tf_op jit(solution)/shard_map/broadcast_in_dim | solution.py:280
  6.4 1.3 %fusion.43 = (pred[1536]{0:T(1024)(128)(4,1)S(1)}, pred[1536]{0:T(1024)(128)(4,1)S(1)}) fusion(s32[]{:T(128)} %bitcast.4, s32[]{:T(128)S(6)} %mul.129, pred[]{:T(512)} %bitcast.5, pred[]{:T(512)} %bitcast.2, s32[]{:T(128)} %bitcast.1), kind=kLoop, calls=%fused_computation.70 | loop fusion | flops 16896 | bytes 3086 | tf_op jit(solution)/shard_map/and | solution.py:266
  7.7 1.3 %fusion.36 = (s32[1536]{0:T(1024)S(1)}, s32[1536]{0:T(1024)S(1)}) fusion(s32[]{:T(128)} %bitcast.1, s32[]{:T(128)S(6)} %mul.129, pred[]{:T(512)} %bitcast.2, pred[]{:T(512)} %bitcast.5, s32[]{:T(128)} %bitcast.4), kind=kLoop, calls=%fused_computation.63 | loop fusion | flops 19968 | bytes 12302 | tf_op jit(solution)/shard_map/jit(_where)/select_n | solution.py:267
  9.0 0.6 fusion.26.onehot_ref
  9.6 0.6 fusion.22
  10.2 0.6 fusion.18
  10.9 0.0 copy-start
  10.9 0.8 pad_maximum_fusion.2.c2_ref
  11.7 0.8 pad_maximum_fusion.1.c1_ref
  12.6 1.7 %sine_negate_fusion.1 = (f32[1,32,1536]{2,1,0:T(8,128)S(1)}, f32[1,32,1536]{2,1,0:T(8,128)S(1)}, f32[1,32,1536]{2,1,0:T(8,128)S(1)}, f32[1,32,1536]{2,1,0:T(8,128)S(1)}) fusion(s32[1536]{0:T(1024)S(1)} %get-tuple-element.31, s32[32]{0:T(128)S(1)} %multiply_add_fusion, s32[1536]{0:T(1024)S(1)} %get-tuple-element.32), kind=kLoop, calls=%fused_computation.23 | loop fusion | flops 983040 | bytes 798848 | tf_op jit(solution)/shard_map/neg | solution.py:245
  14.2 0.8 pad_maximum_fusion.4.ai_ref
  15.0 0.8 pad_maximum_fusion.3.ar_ref
  15.8 0.0 copy-done
  15.8 0.1 select_bitcast_fusion.1
  15.9 0.9 pad_maximum_fusion.x_ref
  16.8 79.1 %shard_map.55 = (f32[8,20,128]{2,1,0:T(8,128)}, f32[8,20,128]{2,1,0:T(8,128)}) custom-call(f32[2,32,1536]{2,1,0:T(8,128)} %pad_maximum_fusion.3.ar_ref, f32[2,32,1536]{2,1,0:T(8,128)} %pad_maximum_fusion.4.ai_ref, f32[2,40,1536]{2,1,0:T(8,128)} %pad_maximum_fusion.1.c1_ref, f32[2,40,1536]{2,1,0:T(8,128)} %pad_maximum_fusion.2.c2_ref, ...), custom_call_target="tpu_custom_call" | custom-call | tf_op jit(solution)/shard_map/pallas_call | solution.py:214
  96.0 0.9 convert_element_type.52
  96.9 0.9 convert_element_type.53
  97.8 0.4 convolution_bitcast_fusion
  98.2 0.4 convolution_bitcast_fusion.1
  98.6 0.3 maximum_multiply_fusion
  99.0 1.7 %copy.11 = f32[20,2,128,128]{3,2,1,0:T(8,128)} copy(f32[20,2,128,128]{3,2,0,1:T(8,128)S(1)} %maximum_multiply_fusion) | data formatting | bytes 5242880 | tf_op jit(solution)/shard_map/div | solution.py:295
  (5 shorter events, 0.1 us)
Async XLA Ops:
  10.9 4.9 %copy-start = (bf16[128,1536]{1,0:T(8,128)(2,1)S(1)}, bf16[128,1536]{1,0:T(8,128)(2,1)}, u32[]{:S(2)}) copy-start(bf16[128,1536]{1,0:T(8,128)(2,1)} %param.5) | copy-start | bytes 1179652

commit v6 on v5

--- a/solution.py
+++ b/solution.py
@@ -179,7 +179,7 @@
             white_ref[2 * w + p] = white
             src_send[2 * w + p] = jnp.dot(
                 white.astype(jnp.bfloat16), onehot, preferred_element_type=jnp.float32
-            )
+            ).astype(jnp.bfloat16)
 
     def srcc(peer, src_dev):
         return pltpu.make_async_remote_copy(
@@ -200,9 +200,9 @@
         src = lax.rem(mc + n_chan - i, n_chan)
         srcc(src, src).wait_recv()
 
-    total = src_recv[0]
+    total = src_recv[0].astype(jnp.float32)
     for s in range(1, n_chan):
-        total = total + src_recv[s]
+        total = total + src_recv[s].astype(jnp.float32)
     srcspec_ref[...] = total
 
 
@@ -226,8 +226,8 @@
             pltpu.VMEM((NWIN, 2 * bins_dev, channels), jnp.float32),
             pltpu.VMEM((8, channels), jnp.float32),
             pltpu.VMEM((n_tm, 8, channels), jnp.float32),
-            pltpu.VMEM((NWIN * 2, bins_dev, nsrc), jnp.float32),
-            pltpu.VMEM((n_chan, NWIN * 2, bins_dev, nsrc), jnp.float32),
+            pltpu.VMEM((NWIN * 2, bins_dev, nsrc), jnp.bfloat16),
+            pltpu.VMEM((n_chan, NWIN * 2, bins_dev, nsrc), jnp.bfloat16),
             pltpu.SemaphoreType.DMA((n_tm, SLOTS)),
             pltpu.SemaphoreType.DMA((n_tm, SLOTS)),
             pltpu.SemaphoreType.DMA((n_tm,)),

time: 101 us -> 88.9 us (0.88)
  the two profiles are of different devices: /device:TPU:166 before, /device:TPU:6 now
where the time goes in v6:
time: 88.9 us; the launch traced here: 88.6 us
  Pallas kernels  67.1 us (75%)
  other arithmetic  14.3 us (16%)
  local copies, waits for them, and re-layouts  4.28 us (5%)
  between operations  2.06 us (2%)
    pallas_call x1, Pallas kernels, fused_exchange(): pl.pallas_call(functools.partial(_fused_kernel, n_tm, n_chan, bins_dev, f...  67.1 us

profile of v6, /device:TPU:6, one launch (start us, length us, event | category | flops | bytes accessed | tf_op | source)
XLA Modules:
  0.0 88.6 jit_solution(9424280545369787138)
XLA Ops:
  0.0 0.7 broadcast_subtract_fusion
  0.7 1.2 %dynamic_slice.9 = s32[1]{0:T(128)} dynamic-slice(s32[32]{0:T(128)} %constant.68.clone, s32[]{:T(128)S(6)} %select_n.74), dynamic_slice_sizes={1} | dynamic-slice | bytes 12 | tf_op jit(solution)/shard_map/dynamic_slice | solution.py:257
  3.9 1.3 %fusion.48 = (s32[1]{0:T(128)}, s32[1]{0:T(128)}) fusion(s32[4]{0:T(128)} %param.6, s32[]{:T(128)S(6)} %select_n.75, s32[]{:T(128)S(6)} %select_n.78), kind=kLoop, calls=%fused_computation.78 | loop fusion | bytes 24 | tf_op jit(solution)/shard_map/dynamic_slice | solution.py:264
  5.2 1.2 %convert_bitcast_fusion.mask_ref = f32[1,128]{1,0:T(1,128)} fusion(s32[128]{0:T(128)} %param.7), kind=kLoop, calls=%fused_computation.73 | loop fusion | flops 128 | bytes 1024 | tf_op jit(solution)/shard_map/broadcast_in_dim | solution.py:280
  6.4 1.3 %fusion.43 = (pred[1536]{0:T(1024)(128)(4,1)S(1)}, pred[1536]{0:T(1024)(128)(4,1)S(1)}) fusion(s32[]{:T(128)} %bitcast.4, s32[]{:T(128)S(6)} %mul.129, pred[]{:T(512)} %bitcast.5, pred[]{:T(512)} %bitcast.2, s32[]{:T(128)} %bitcast.1), kind=kLoop, calls=%fused_computation.70 | loop fusion | flops 16896 | bytes 3086 | tf_op jit(solution)/shard_map/and | solution.py:266
  7.7 1.3 %fusion.36 = (s32[1536]{0:T(1024)S(1)}, s32[1536]{0:T(1024)S(1)}) fusion(s32[]{:T(128)} %bitcast.1, s32[]{:T(128)S(6)} %mul.129, pred[]{:T(512)} %bitcast.2, pred[]{:T(512)} %bitcast.5, s32[]{:T(128)} %bitcast.4), kind=kLoop, calls=%fused_computation.63 | loop fusion | flops 19968 | bytes 12302 | tf_op jit(solution)/shard_map/jit(_where)/select_n | solution.py:267
  9.0 0.6 fusion.26.onehot_ref
  9.6 0.6 fusion.22
  10.2 0.6 fusion.18
  10.9 0.0 copy-start
  10.9 0.8 pad_maximum_fusion.2.c2_ref
  11.7 0.8 pad_maximum_fusion.1.c1_ref
  12.6 1.7 %sine_negate_fusion.1 = (f32[1,32,1536]{2,1,0:T(8,128)S(1)}, f32[1,32,1536]{2,1,0:T(8,128)S(1)}, f32[1,32,1536]{2,1,0:T(8,128)S(1)}, f32[1,32,1536]{2,1,0:T(8,128)S(1)}) fusion(s32[1536]{0:T(1024)S(1)} %get-tuple-element.31, s32[32]{0:T(128)S(1)} %multiply_add_fusion, s32[1536]{0:T(1024)S(1)} %get-tuple-element.32), kind=kLoop, calls=%fused_computation.23 | loop fusion | flops 983040 | bytes 798848 | tf_op jit(solution)/shard_map/neg | solution.py:245
  14.2 0.8 pad_maximum_fusion.4.ai_ref
  15.0 0.8 pad_maximum_fusion.3.ar_ref
  15.8 0.0 copy-done
  15.8 0.1 select_bitcast_fusion.1
  15.9 0.9 %pad_maximum_fusion.x_ref = bf16[2,128,1536]{2,1,0:T(8,128)(2,1)} fusion(bf16[1,128,1536]{2,1,0:T(8,128)(2,1)S(1)} %get-tuple-element.10, bf16[1,128,1536]{2,1,0:T(8,128)(2,1)S(1)} %get-tuple-element.9), kind=kLoop, calls=%fused_computation.3 | loop fusion | flops 393216 | bytes 1572864 | tf_op jit(solution)/shard_map/stack | solution.py:282
  16.8 67.1 %shard_map.55 = (f32[8,20,128]{2,1,0:T(8,128)}, f32[8,20,128]{2,1,0:T(8,128)}) custom-call(f32[2,32,1536]{2,1,0:T(8,128)} %pad_maximum_fusion.3.ar_ref, f32[2,32,1536]{2,1,0:T(8,128)} %pad_maximum_fusion.4.ai_ref, f32[2,40,1536]{2,1,0:T(8,128)} %pad_maximum_fusion.1.c1_ref, f32[2,40,1536]{2,1,0:T(8,128)} %pad_maximum_fusion.2.c2_ref, ...), custom_call_target="tpu_custom_call" | custom-call | tf_op jit(solution)/shard_map/pallas_call | solution.py:214
  83.9 0.9 %convert_element_type.52 = bf16[8,20,128]{2,1,0:T(8,128)(2,1)S(1)} convert(f32[8,20,128]{2,1,0:T(8,128)} %get-tuple-element.7) | non-fusion elementwise | flops 20480 | bytes 122880 | tf_op jit(solution)/shard_map/convert_element_type | solution.py:286
  84.8 0.9 %convert_element_type.53 = bf16[8,20,128]{2,1,0:T(8,128)(2,1)S(1)} convert(f32[8,20,128]{2,1,0:T(8,128)} %get-tuple-element.8) | non-fusion elementwise | flops 20480 | bytes 122880 | tf_op jit(solution)/shard_map/convert_element_type | solution.py:287
  85.8 0.4 convolution_bitcast_fusion
  86.2 0.4 convolution_bitcast_fusion.1
  86.6 0.3 maximum_multiply_fusion
  86.9 1.7 %copy.11 = f32[20,2,128,128]{3,2,1,0:T(8,128)} copy(f32[20,2,128,128]{3,2,0,1:T(8,128)S(1)} %maximum_multiply_fusion) | data formatting | bytes 5242880 | tf_op jit(solution)/shard_map/div | solution.py:295
  (5 shorter events, 0.1 us)
Async XLA Ops:
  10.9 4.9 %copy-start = (bf16[128,1536]{1,0:T(8,128)(2,1)S(1)}, bf16[128,1536]{1,0:T(8,128)(2,1)}, u32[]{:S(2)}) copy-start(bf16[128,1536]{1,0:T(8,128)(2,1)} %param.5) | copy-start | bytes 1179652

commit v7 on v6

--- a/solution.py
+++ b/solution.py
@@ -41,8 +41,9 @@
 
 
 def _fused_kernel(n_tm, n_chan, bins_dev, first, count,
-                  ar_ref, ai_ref, c1_ref, c2_ref, x_ref, onehot_ref, mask_ref,
+                  offsets_ref, record_ref, dead_ref, sources_ref,
                   white_ref, srcspec_ref,
+                  ar_ref, ai_ref, c1_ref, c2_ref, x_ref,
                   blocks_ref, lhs, recv, spec, lvl_send, lvl_recv, src_send, src_recv,
                   a2a_send_sem, a2a_recv_sem, lvl_send_sem, lvl_recv_sem,
                   src_send_sem, src_recv_sem):
@@ -60,6 +61,38 @@
     for i in range(1, n_chan):
         pl.semaphore_signal(barrier, inc=1, device_id={"chan": lax.rem(mc + i, n_chan)},
                             device_id_type=MESH)
+
+    span = record_ref.shape[1]
+    wa = jnp.int32(0)
+    for d in range(n_tm):
+        wa = jnp.where(me == d, first[d], wa)
+    local_times = me * span + lax.broadcasted_iota(jnp.int32, (1, span), 1)
+    coarse = FLO + bins_dev * lax.broadcasted_iota(jnp.int32, (n_tm, 1), 0)
+    fine_row = lax.broadcasted_iota(jnp.int32, (2 * bins_dev, 1), 0)
+    fine = lax.rem(fine_row, bins_dev)
+    scale = 2.0 * math.pi / W
+
+    def prepare(slot):
+        window = wa + slot
+        origin = offsets_ref[jnp.minimum(window, NWIN - 1)]
+        shifted = local_times - origin
+        inside = (shifted >= 0) & (shifted < W) & (window < NWIN)
+        times = jnp.where(inside, shifted, 0)
+        angle = lax.rem(coarse * times, W).astype(jnp.float32) * scale
+        ar_ref[slot] = jnp.cos(angle)
+        ai_ref[slot] = -jnp.sin(angle)
+        angle = lax.rem(fine * times, W).astype(jnp.float32) * scale
+        cos, sin = jnp.cos(angle), jnp.sin(angle)
+        top = fine_row < bins_dev
+        c1_ref[slot] = jnp.where(top, cos, -sin)
+        c2_ref[slot] = jnp.where(top, sin, cos)
+        x_ref[slot] = jnp.where(inside, record_ref[...], jnp.zeros_like(record_ref[...]))
+
+    prepare(0)
+
+    @pl.when(me_two)
+    def _():
+        prepare(1)
 
     def a2a(peer, slot, src_dev):
         return pltpu.make_async_remote_copy(
@@ -167,8 +200,11 @@
         level = level + lvl_recv[s]
     level = level / F
 
-    mask = mask_ref[...]
-    onehot = onehot_ref[...]
+    mask = dead_ref[...].astype(jnp.float32)
+    channels = record_ref.shape[0]
+    local_index = sources_ref[...] - mc * channels
+    onehot = (lax.broadcasted_iota(jnp.int32, (channels, local_index.shape[1]), 0)
+              == local_index).astype(jnp.bfloat16)
     for w in range(NWIN):
         re = spec[w, 0:bins_dev, :]
         im = spec[w, bins_dev:2 * bins_dev, :]
@@ -206,9 +242,9 @@
     srcspec_ref[...] = total
 
 
-def fused_exchange(ar, ai, c1, c2, x, onehot, mask, n_tm, n_chan, bins_dev, first, count):
-    channels, span = x.shape[1], x.shape[2]
-    nsrc = onehot.shape[1]
+def fused_exchange(offsets, record, dead, sources, n_tm, n_chan, bins_dev, first, count):
+    channels, span = record.shape
+    nsrc = sources.shape[1]
     group = 8
     vmem = pl.BlockSpec(memory_space=pltpu.VMEM)
     return pl.pallas_call(
@@ -217,9 +253,14 @@
             jax.ShapeDtypeStruct((NWIN * 2, bins_dev, channels), jnp.float32),
             jax.ShapeDtypeStruct((NWIN * 2, bins_dev, nsrc), jnp.float32),
         ),
-        in_specs=[vmem] * 7,
+        in_specs=[pl.BlockSpec(memory_space=pltpu.SMEM), vmem, vmem, vmem],
         out_specs=(vmem, vmem),
         scratch_shapes=[
+            pltpu.VMEM((SLOTS, n_tm, span), jnp.float32),
+            pltpu.VMEM((SLOTS, n_tm, span), jnp.float32),
+            pltpu.VMEM((SLOTS, 2 * bins_dev, span), jnp.float32),
+            pltpu.VMEM((SLOTS, 2 * bins_dev, span), jnp.float32),
+            pltpu.VMEM((SLOTS, channels, span), jnp.bfloat16),
             pltpu.VMEM((n_tm, SLOTS, 2 * bins_dev, channels), jnp.float32),
             pltpu.VMEM((group * 2 * bins_dev, span), jnp.float32),
             pltpu.VMEM((n_tm, SLOTS, 2 * bins_dev, channels), jnp.float32),
@@ -236,13 +277,7 @@
             pltpu.SemaphoreType.DMA((n_chan,)),
         ],
         compiler_params=pltpu.CompilerParams(collective_id=0, has_side_effects=True),
-    )(ar, ai, c1, c2, x, onehot, mask)
-
-
-def phasor(bins, times):
-    phase = bins[:, None] * times[None, :] % W
-    angle = phase.astype(jnp.float32) * (2.0 * math.pi / W)
-    return jnp.cos(angle), -jnp.sin(angle)
+    )(offsets, record, dead, sources)
 
 
 def shards(record, offsets, dead_mask, sources):
@@ -251,36 +286,9 @@
     bins_dev = F // n_tm
     channels, span = record.shape
     first, count = window_plan(n_tm, span)
-    me = lax.axis_index("tm")
-    start = me * span
-    local_times = start + jnp.arange(span, dtype=jnp.int32)
-    wa = jnp.asarray(first, jnp.int32)[me]
-    coarse = FLO + bins_dev * jnp.arange(n_tm, dtype=jnp.int32)
-    fine = jnp.arange(bins_dev, dtype=jnp.int32)
-
-    ars, ais, c1s, c2s, xs = [], [], [], [], []
-    for slot in range(SLOTS):
-        window = wa + slot
-        origin = offsets[jnp.minimum(window, NWIN - 1)]
-        shifted = local_times - origin
-        inside = (shifted >= 0) & (shifted < W) & (window < NWIN)
-        times = jnp.where(inside, shifted, 0)
-        ar, ai = phasor(coarse, times)
-        br, bi = phasor(fine, times)
-        ars.append(ar)
-        ais.append(ai)
-        c1s.append(jnp.concatenate([br, bi], axis=0))
-        c2s.append(jnp.concatenate([-bi, br], axis=0))
-        xs.append(jnp.where(inside[None, :], record, jnp.zeros_like(record)))
-
-    local_index = sources - lax.axis_index("chan") * channels
-    onehot = (jnp.arange(channels, dtype=jnp.int32)[:, None] == local_index[None, :]).astype(
-        jnp.bfloat16
-    )
-    mask = dead_mask.astype(jnp.float32)[None, :]
     white, source_spec = fused_exchange(
-        jnp.stack(ars), jnp.stack(ais), jnp.stack(c1s), jnp.stack(c2s), jnp.stack(xs),
-        onehot, mask, n_tm, n_chan, bins_dev, first, count
+        offsets, record, dead_mask.reshape(1, channels), sources.reshape(1, -1),
+        n_tm, n_chan, bins_dev, first, count
     )
 
     left = source_spec.astype(jnp.bfloat16).reshape(NWIN, 2, bins_dev, -1)

time: 88.9 us -> 71.4 us (0.80)
  other arithmetic: 14.3 us -> 2.12 us
  local copies, waits for them, and re-layouts: 4.28 us -> 1.69 us
  between operations: 2.06 us -> 0.04 us
    another operation x8 -> x0, other arithmetic: 4.3 us -> none  [the longest x2 1.01 us: shards(): jnp.stack(xs)]
    dynamic_slice x2 -> x0, local copies, waits for them, and re-layouts: 2.58 us -> none  [the longest x1 1.35 us: shards(): origin = offsets[jnp.minimum(window, NWIN - 1)]]
    neg x1 -> x0, other arithmetic: 1.66 us -> none  [phasor(): return (jnp.cos(angle), -jnp.sin(angle))]
    and x1 -> x0, other arithmetic: 1.29 us -> none  [shards(): inside = (shifted >= 0) & (shifted < W) & (window < NWIN)]
    select_n x1 -> x0, other arithmetic: 1.29 us -> none  [shards(): times = jnp.where(inside, shifted, 0)]
    sin x2 -> x0, other arithmetic: 1.23 us -> none  [phasor(): return (jnp.cos(angle), -jnp.sin(angle))]
    broadcast_in_dim x1 -> x0, other arithmetic: 1.16 us -> none  [shards(): mask = dead_mask.astype(jnp.float32)[None, :]]
where the time goes in v7:
time: 71.4 us; the launch traced here: 71.2 us
  Pallas kernels  66.6 us (93%)
  other arithmetic  2.12 us (3%)
  local copies, waits for them, and re-layouts  1.69 us (2%)
  matrix products  0.81 us (1%)
    pallas_call x1, Pallas kernels, fused_exchange(): pl.pallas_call(functools.partial(_fused_kernel, n_tm, n_chan, bins_dev, f...  66.6 us
    div x1, local copies, waits for them, and re-layouts, shards(): return jnp.stack([real_component, imaginary_component], axis=1) / NWIN  1.67 us

profile of v7, /device:TPU:6, one launch (start us, length us, event | category | flops | bytes accessed | tf_op | source)
XLA Modules:
  0.0 71.2 jit_solution(706875865105467281)
XLA Ops:
  0.0 66.6 %shard_map.46 = (f32[8,20,128]{2,1,0:T(8,128)}, f32[8,20,128]{2,1,0:T(8,128)}) custom-call(s32[4]{0:T(128)} %offsets_ref.1, bf16[128,1536]{1,0:T(8,128)(2,1)} %record_ref.1, s32[1,128]{1,0:T(1,128)} %bitcast.16, s32[1,128]{1,0:T(1,128)} %bitcast.17), custom_call_target="tpu_custom_call" | custom-call | tf_op jit(solution)/shard_map/pallas_call | solution.py:250
  66.6 0.9 %convert_element_type.6 = bf16[8,20,128]{2,1,0:T(8,128)(2,1)S(1)} convert(f32[8,20,128]{2,1,0:T(8,128)} %get-tuple-element.7) | non-fusion elementwise | flops 20480 | bytes 122880 | tf_op jit(solution)/shard_map/convert_element_type | solution.py:294
  67.5 0.9 %convert_element_type.7 = bf16[8,20,128]{2,1,0:T(8,128)(2,1)S(1)} convert(f32[8,20,128]{2,1,0:T(8,128)} %get-tuple-element.8) | non-fusion elementwise | flops 20480 | bytes 122880 | tf_op jit(solution)/shard_map/convert_element_type | solution.py:295
  68.4 0.4 convolution_bitcast_fusion
  68.8 0.4 convolution_bitcast_fusion.1
  69.3 0.3 maximum_multiply_fusion
  69.6 1.7 %copy.10 = f32[20,2,128,128]{3,2,1,0:T(8,128)} copy(f32[20,2,128,128]{3,2,0,1:T(8,128)S(1)} %maximum_multiply_fusion) | data formatting | bytes 5242880 | tf_op jit(solution)/shard_map/div | solution.py:303
  (2 shorter events, 0.0 us)

commit v8 on v7

--- a/solution.py
+++ b/solution.py
@@ -44,9 +44,9 @@
                   offsets_ref, record_ref, dead_ref, sources_ref,
                   white_ref, srcspec_ref,
                   ar_ref, ai_ref, c1_ref, c2_ref, x_ref,
-                  blocks_ref, lhs, recv, spec, lvl_send, lvl_recv, src_send, src_recv,
+                  blocks_ref, lhs, recv, spec, lvl_send, lvl_recv, src_send,
                   a2a_send_sem, a2a_recv_sem, lvl_send_sem, lvl_recv_sem,
-                  src_send_sem, src_recv_sem):
+                  src_send_sem, src_recv_sem, rs_recv, ag_send, ag_send_sem, ag_recv_sem):
     me = lax.axis_index("tm")
     mc = lax.axis_index("chan")
     two = [d for d in range(n_tm) if count[d] == 2]
@@ -205,6 +205,9 @@
     local_index = sources_ref[...] - mc * channels
     onehot = (lax.broadcasted_iota(jnp.int32, (channels, local_index.shape[1]), 0)
               == local_index).astype(jnp.bfloat16)
+    per = NWIN * 2 * bins_dev // n_chan
+    halves = bins_dev // per
+    src_send[...] = jnp.zeros_like(src_send)
     for w in range(NWIN):
         re = spec[w, 0:bins_dev, :]
         im = spec[w, bins_dev:2 * bins_dev, :]
@@ -213,14 +216,16 @@
         for p, part in enumerate((re, im)):
             white = (part / den).astype(jnp.bfloat16).astype(jnp.float32) * mask
             white_ref[2 * w + p] = white
-            src_send[2 * w + p] = jnp.dot(
+            picked = jnp.dot(
                 white.astype(jnp.bfloat16), onehot, preferred_element_type=jnp.float32
-            ).astype(jnp.bfloat16)
-
-    def srcc(peer, src_dev):
+            )
+            for h in range(halves):
+                src_send[(2 * w + p) * halves + h, 0:per, :] = picked[h * per:(h + 1) * per, :]
+
+    def rsc(peer, src_dev):
         return pltpu.make_async_remote_copy(
-            src_ref=src_send,
-            dst_ref=src_recv.at[src_dev],
+            src_ref=src_send.at[peer],
+            dst_ref=rs_recv.at[src_dev],
             send_sem=src_send_sem.at[peer],
             recv_sem=src_recv_sem.at[src_dev],
             device_id={"chan": peer},
@@ -228,18 +233,37 @@
         )
 
     for i in range(1, n_chan):
-        srcc(lax.rem(mc + i, n_chan), mc).start()
-    src_recv[mc] = src_send[...]
-    for i in range(1, n_chan):
-        srcc(lax.rem(mc + i, n_chan), mc).wait_send()
+        rsc(lax.rem(mc + i, n_chan), mc).start()
+    rs_recv[mc] = src_send[mc]
+    for i in range(1, n_chan):
+        rsc(lax.rem(mc + i, n_chan), mc).wait_send()
     for i in range(1, n_chan):
         src = lax.rem(mc + n_chan - i, n_chan)
-        srcc(src, src).wait_recv()
-
-    total = src_recv[0].astype(jnp.float32)
+        rsc(src, src).wait_recv()
+
+    total = rs_recv[0]
     for s in range(1, n_chan):
-        total = total + src_recv[s].astype(jnp.float32)
-    srcspec_ref[...] = total
+        total = total + rs_recv[s]
+    ag_send[...] = total
+
+    def agc(peer, src_dev):
+        return pltpu.make_async_remote_copy(
+            src_ref=ag_send,
+            dst_ref=srcspec_ref.at[src_dev],
+            send_sem=ag_send_sem.at[peer],
+            recv_sem=ag_recv_sem.at[src_dev],
+            device_id={"chan": peer},
+            device_id_type=MESH,
+        )
+
+    for i in range(1, n_chan):
+        agc(lax.rem(mc + i, n_chan), mc).start()
+    srcspec_ref[mc] = ag_send[...]
+    for i in range(1, n_chan):
+        agc(lax.rem(mc + i, n_chan), mc).wait_send()
+    for i in range(1, n_chan):
+        src = lax.rem(mc + n_chan - i, n_chan)
+        agc(src, src).wait_recv()
 
 
 def fused_exchange(offsets, record, dead, sources, n_tm, n_chan, bins_dev, first, count):
@@ -251,7 +275,7 @@
         functools.partial(_fused_kernel, n_tm, n_chan, bins_dev, first, count),
         out_shape=(
             jax.ShapeDtypeStruct((NWIN * 2, bins_dev, channels), jnp.float32),
-            jax.ShapeDtypeStruct((NWIN * 2, bins_dev, nsrc), jnp.float32),
+            jax.ShapeDtypeStruct((n_chan, 16, nsrc), jnp.float32),
         ),
         in_specs=[pl.BlockSpec(memory_space=pltpu.SMEM), vmem, vmem, vmem],
         out_specs=(vmem, vmem),
@@ -267,12 +291,15 @@
             pltpu.VMEM((NWIN, 2 * bins_dev, channels), jnp.float32),
             pltpu.VMEM((8, channels), jnp.float32),
             pltpu.VMEM((n_tm, 8, channels), jnp.float32),
-            pltpu.VMEM((NWIN * 2, bins_dev, nsrc), jnp.bfloat16),
-            pltpu.VMEM((n_chan, NWIN * 2, bins_dev, nsrc), jnp.bfloat16),
+            pltpu.VMEM((n_chan, 16, nsrc), jnp.float32),
             pltpu.SemaphoreType.DMA((n_tm, SLOTS)),
             pltpu.SemaphoreType.DMA((n_tm, SLOTS)),
             pltpu.SemaphoreType.DMA((n_tm,)),
             pltpu.SemaphoreType.DMA((n_tm,)),
+            pltpu.SemaphoreType.DMA((n_chan,)),
+            pltpu.SemaphoreType.DMA((n_chan,)),
+            pltpu.VMEM((n_chan, 16, nsrc), jnp.float32),
+            pltpu.VMEM((16, nsrc), jnp.float32),
             pltpu.SemaphoreType.DMA((n_chan,)),
             pltpu.SemaphoreType.DMA((n_chan,)),
         ],
@@ -291,7 +318,9 @@
         n_tm, n_chan, bins_dev, first, count
     )
 
-    left = source_spec.astype(jnp.bfloat16).reshape(NWIN, 2, bins_dev, -1)
+    per = NWIN * 2 * bins_dev // n_chan
+    assert per * n_chan == NWIN * 2 * bins_dev and bins_dev % per == 0 and per <= 16
+    left = source_spec[:, :per].astype(jnp.bfloat16).reshape(NWIN, 2, bins_dev, -1)
     right = white.astype(jnp.bfloat16).reshape(NWIN, 2, bins_dev, channels)
     right_imaginary = jnp.stack([right[:, 1], -right[:, 0]], axis=1)
     real_component = jnp.einsum(

time: 71.4 us -> 64.5 us (0.903)
  the two profiles are of different devices: /device:TPU:6 before, /device:TPU:1 now
where the time goes in v8:
time: 64.5 us; the launch traced here: 64.4 us
  Pallas kernels  59.7 us (93%)
  local copies, waits for them, and re-layouts  2.62 us (4%)
  other arithmetic  1.22 us (2%)
  matrix products  0.81 us (1%)
    pallas_call x1, Pallas kernels, fused_exchange(): pl.pallas_call(functools.partial(_fused_kernel, n_tm, n_chan, bins_dev, f...  59.7 us
    div x1, local copies, waits for them, and re-layouts, shards(): return jnp.stack([real_component, imaginary_component], axis=1) / NWIN  1.67 us

profile of v8, /device:TPU:1, one launch (start us, length us, event | category | flops | bytes accessed | tf_op | source)
XLA Modules:
  0.0 64.4 jit_solution(6314936942715357008)
XLA Ops:
  0.0 59.7 %shard_map.46 = (f32[8,20,128]{2,1,0:T(8,128)}, f32[16,16,128]{2,1,0:T(8,128)}) custom-call(s32[4]{0:T(128)} %offsets_ref.1, bf16[128,1536]{1,0:T(8,128)(2,1)} %record_ref.1, s32[1,128]{1,0:T(1,128)} %bitcast.13, s32[1,128]{1,0:T(1,128)} %bitcast.14), custom_call_target="tpu_custom_call" | custom-call | tf_op jit(solution)/shard_map/pallas_call | solution.py:274
  59.7 0.9 %slice.18 = bf16[16,10,128]{2,1,0:T(8,128)(2,1)S(1)} slice(f32[16,16,128]{2,1,0:T(8,128)} %get-tuple-element.7), slice={[0:16], [0:10], [0:128]} | slice | bytes 81920 | tf_op jit(solution)/shard_map/slice | solution.py:323
  60.6 0.9 %convert_element_type.4 = bf16[8,20,128]{2,1,0:T(8,128)(2,1)S(1)} convert(f32[8,20,128]{2,1,0:T(8,128)} %get-tuple-element.8) | non-fusion elementwise | flops 20480 | bytes 122880 | tf_op jit(solution)/shard_map/convert_element_type | solution.py:324
  61.6 0.4 convolution_bitcast_fusion
  62.0 0.4 convolution_bitcast_fusion.1
  62.4 0.3 maximum_multiply_fusion
  62.7 1.7 %copy.16 = f32[20,2,128,128]{3,2,1,0:T(8,128)} copy(f32[20,2,128,128]{3,2,0,1:T(8,128)S(1)} %maximum_multiply_fusion) | data formatting | bytes 5242880 | tf_op jit(solution)/shard_map/div | solution.py:332
  (3 shorter events, 0.1 us)

commit v9 on v8

--- a/solution.py
+++ b/solution.py
@@ -33,6 +33,14 @@
     return first, count
 
 
+def _ring_order(n):
+    order = [0]
+    for i in range(1, n):
+        order.append((i + 1) // 2 if i % 2 else n - i // 2)
+    assert sorted(order) == list(range(n))
+    return order
+
+
 def _any_of(me, members):
     hit = jnp.bool_(False)
     for m in members:
@@ -54,12 +62,14 @@
     rows = 2 * bins_dev
     group = lhs.shape[0] // rows
 
+    order = _ring_order(n_tm)
+    corder = _ring_order(n_chan)
     barrier = pltpu.get_barrier_semaphore()
     for i in range(1, n_tm):
-        pl.semaphore_signal(barrier, inc=1, device_id={"tm": lax.rem(me + i, n_tm)},
+        pl.semaphore_signal(barrier, inc=1, device_id={"tm": lax.rem(me + order[i], n_tm)},
                             device_id_type=MESH)
     for i in range(1, n_chan):
-        pl.semaphore_signal(barrier, inc=1, device_id={"chan": lax.rem(mc + i, n_chan)},
+        pl.semaphore_signal(barrier, inc=1, device_id={"chan": lax.rem(mc + corder[i], n_chan)},
                             device_id_type=MESH)
 
     span = record_ref.shape[1]
@@ -108,7 +118,7 @@
         c1 = c1_ref[slot]
         c2 = c2_ref[slot]
         for dd in range(group):
-            d = lax.rem(me + g * group + dd, n_tm)
+            d = lax.rem(me + order[g * group + dd], n_tm)
             ar = ar_ref[slot, pl.ds(d, 1), :]
             ai = ai_ref[slot, pl.ds(d, 1), :]
             lhs[dd * rows:(dd + 1) * rows, :] = ar * c1 + ai * c2
@@ -117,24 +127,28 @@
             preferred_element_type=jnp.float32,
         )
         for dd in range(group):
-            d = lax.rem(me + g * group + dd, n_tm)
+            d = lax.rem(me + order[g * group + dd], n_tm)
             blocks_ref[d, slot] = res[dd * rows:(dd + 1) * rows, :]
 
     def send(g, slot):
         for dd in range(group):
             if g == 0 and dd == 0:
                 continue
-            a2a(lax.rem(me + g * group + dd, n_tm), slot, me).start()
+            a2a(lax.rem(me + order[g * group + dd], n_tm), slot, me).start()
 
     for g in range(n_tm // group):
         compute(g, 0)
-        if g == 0:
-            pl.semaphore_wait(barrier, n_tm - 1 + n_chan - 1)
-        send(g, 0)
 
         @pl.when(me_two)
         def _():
             compute(g, 1)
+
+    pl.semaphore_wait(barrier, n_tm - 1 + n_chan - 1)
+    for g in range(n_tm // group):
+        send(g, 0)
+
+        @pl.when(me_two)
+        def _():
             send(g, 1)
 
     recv[me, 0] = blocks_ref[me, 0]
@@ -144,7 +158,7 @@
         recv[me, 1] = blocks_ref[me, 1]
 
     for i in range(1, n_tm):
-        peer = lax.rem(me + i, n_tm)
+        peer = lax.rem(me + order[i], n_tm)
         a2a(peer, 0, me).wait_send()
 
         @pl.when(me_two)
@@ -187,10 +201,10 @@
         )
 
     for i in range(1, n_tm):
-        lvl(lax.rem(me + i, n_tm), me).start()
+        lvl(lax.rem(me + order[i], n_tm), me).start()
     lvl_recv[me] = lvl_send[...]
     for i in range(1, n_tm):
-        lvl(lax.rem(me + i, n_tm), me).wait_send()
+        lvl(lax.rem(me + order[i], n_tm), me).wait_send()
     for i in range(1, n_tm):
         src = lax.rem(me + n_tm - i, n_tm)
         lvl(src, src).wait_recv()
@@ -233,10 +247,10 @@
         )
 
     for i in range(1, n_chan):
-        rsc(lax.rem(mc + i, n_chan), mc).start()
+        rsc(lax.rem(mc + corder[i], n_chan), mc).start()
     rs_recv[mc] = src_send[mc]
     for i in range(1, n_chan):
-        rsc(lax.rem(mc + i, n_chan), mc).wait_send()
+        rsc(lax.rem(mc + corder[i], n_chan), mc).wait_send()
     for i in range(1, n_chan):
         src = lax.rem(mc + n_chan - i, n_chan)
         rsc(src, src).wait_recv()
@@ -257,10 +271,10 @@
         )
 
     for i in range(1, n_chan):
-        agc(lax.rem(mc + i, n_chan), mc).start()
+        agc(lax.rem(mc + corder[i], n_chan), mc).start()
     srcspec_ref[mc] = ag_send[...]
     for i in range(1, n_chan):
-        agc(lax.rem(mc + i, n_chan), mc).wait_send()
+        agc(lax.rem(mc + corder[i], n_chan), mc).wait_send()
     for i in range(1, n_chan):
         src = lax.rem(mc + n_chan - i, n_chan)
         agc(src, src).wait_recv()

time: 64.5 us -> 66 us (1.023)
  Pallas kernels: 59.7 us -> 60.9 us
    pallas_call x1, Pallas kernels: 59.7 us -> 60.9 us  [fused_exchange(): pl.pallas_call(functools.partial(_fused_kernel, n_tm, n_chan, bins_dev, f...]
where the time goes in v9:
time: 66 us; the launch traced here: 65.6 us
  Pallas kernels  60.9 us (92%)
  local copies, waits for them, and re-layouts  2.62 us (4%)
  other arithmetic  1.22 us (2%)
  matrix products  0.81 us (1%)
    pallas_call x1, Pallas kernels, fused_exchange(): pl.pallas_call(functools.partial(_fused_kernel, n_tm, n_chan, bins_dev, f...  60.9 us
    div x1, local copies, waits for them, and re-layouts, shards(): return jnp.stack([real_component, imaginary_component], axis=1) / NWIN  1.67 us

profile of v9, /device:TPU:1, one launch (start us, length us, event | category | flops | bytes accessed | tf_op | source)
XLA Modules:
  0.0 65.6 jit_solution(3603004951895635568)
XLA Ops:
  0.0 60.9 %shard_map.46 = (f32[8,20,128]{2,1,0:T(8,128)}, f32[16,16,128]{2,1,0:T(8,128)}) custom-call(s32[4]{0:T(128)} %offsets_ref.1, bf16[128,1536]{1,0:T(8,128)(2,1)} %record_ref.1, s32[1,128]{1,0:T(1,128)} %bitcast.13, s32[1,128]{1,0:T(1,128)} %bitcast.14), custom_call_target="tpu_custom_call" | custom-call | tf_op jit(solution)/shard_map/pallas_call | solution.py:288
  60.9 0.9 %slice.18 = bf16[16,10,128]{2,1,0:T(8,128)(2,1)S(1)} slice(f32[16,16,128]{2,1,0:T(8,128)} %get-tuple-element.7), slice={[0:16], [0:10], [0:128]} | slice | bytes 81920 | tf_op jit(solution)/shard_map/slice | solution.py:337
  61.8 0.9 %convert_element_type.4 = bf16[8,20,128]{2,1,0:T(8,128)(2,1)S(1)} convert(f32[8,20,128]{2,1,0:T(8,128)} %get-tuple-element.8) | non-fusion elementwise | flops 20480 | bytes 122880 | tf_op jit(solution)/shard_map/convert_element_type | solution.py:338
  62.8 0.4 convolution_bitcast_fusion
  63.2 0.4 convolution_bitcast_fusion.1
  63.6 0.3 maximum_multiply_fusion
  63.9 1.7 %copy.16 = f32[20,2,128,128]{3,2,1,0:T(8,128)} copy(f32[20,2,128,128]{3,2,0,1:T(8,128)S(1)} %maximum_multiply_fusion) | data formatting | bytes 5242880 | tf_op jit(solution)/shard_map/div | solution.py:346
  (3 shorter events, 0.1 us)

commit v10 on v9

--- a/solution.py
+++ b/solution.py
@@ -138,17 +138,13 @@
 
     for g in range(n_tm // group):
         compute(g, 0)
+        if g == 0:
+            pl.semaphore_wait(barrier, n_tm - 1 + n_chan - 1)
+        send(g, 0)
 
         @pl.when(me_two)
         def _():
             compute(g, 1)
-
-    pl.semaphore_wait(barrier, n_tm - 1 + n_chan - 1)
-    for g in range(n_tm // group):
-        send(g, 0)
-
-        @pl.when(me_two)
-        def _():
             send(g, 1)
 
     recv[me, 0] = blocks_ref[me, 0]

time: 66 us -> 65.9 us (level)
  no operation moved by 1% of the time
where the time goes in v10:
time: 65.9 us; the launch traced here: 65.2 us
  Pallas kernels  60.5 us (92%)
  local copies, waits for them, and re-layouts  2.62 us (4%)
  other arithmetic  1.22 us (2%)
  matrix products  0.81 us (1%)
    pallas_call x1, Pallas kernels, fused_exchange(): pl.pallas_call(functools.partial(_fused_kernel, n_tm, n_chan, bins_dev, f...  60.5 us
    div x1, local copies, waits for them, and re-layouts, shards(): return jnp.stack([real_component, imaginary_component], axis=1) / NWIN  1.67 us

profile of v10, /device:TPU:1, one launch (start us, length us, event | category | flops | bytes accessed | tf_op | source)
XLA Modules:
  0.0 65.2 jit_solution(17919864027119586645)
XLA Ops:
  0.0 60.5 %shard_map.46 = (f32[8,20,128]{2,1,0:T(8,128)}, f32[16,16,128]{2,1,0:T(8,128)}) custom-call(s32[4]{0:T(128)} %offsets_ref.1, bf16[128,1536]{1,0:T(8,128)(2,1)} %record_ref.1, s32[1,128]{1,0:T(1,128)} %bitcast.13, s32[1,128]{1,0:T(1,128)} %bitcast.14), custom_call_target="tpu_custom_call" | custom-call | tf_op jit(solution)/shard_map/pallas_call | solution.py:284
  60.5 0.9 %slice.18 = bf16[16,10,128]{2,1,0:T(8,128)(2,1)S(1)} slice(f32[16,16,128]{2,1,0:T(8,128)} %get-tuple-element.7), slice={[0:16], [0:10], [0:128]} | slice | bytes 81920 | tf_op jit(solution)/shard_map/slice | solution.py:333
  61.5 0.9 %convert_element_type.4 = bf16[8,20,128]{2,1,0:T(8,128)(2,1)S(1)} convert(f32[8,20,128]{2,1,0:T(8,128)} %get-tuple-element.8) | non-fusion elementwise | flops 20480 | bytes 122880 | tf_op jit(solution)/shard_map/convert_element_type | solution.py:334
  62.4 0.4 convolution_bitcast_fusion
  62.8 0.4 convolution_bitcast_fusion.1
  63.2 0.3 maximum_multiply_fusion
  63.5 1.7 %copy.16 = f32[20,2,128,128]{3,2,1,0:T(8,128)} copy(f32[20,2,128,128]{3,2,0,1:T(8,128)S(1)} %maximum_multiply_fusion) | data formatting | bytes 5242880 | tf_op jit(solution)/shard_map/div | solution.py:342
  (3 shorter events, 0.1 us)

commit v11 on v8

--- a/solution.py
+++ b/solution.py
@@ -46,7 +46,8 @@
                   ar_ref, ai_ref, c1_ref, c2_ref, x_ref,
                   blocks_ref, lhs, recv, spec, lvl_send, lvl_recv, src_send,
                   a2a_send_sem, a2a_recv_sem, lvl_send_sem, lvl_recv_sem,
-                  src_send_sem, src_recv_sem, rs_recv, ag_send, ag_send_sem, ag_recv_sem):
+                  src_send_sem, src_recv_sem, rs_recv, ag_send, ag_send_sem, ag_recv_sem,
+                  ag_recv):
     me = lax.axis_index("tm")
     mc = lax.axis_index("chan")
     two = [d for d in range(n_tm) if count[d] == 2]
@@ -215,7 +216,7 @@
         den = mag + 0.1 * level[w:w + 1, :] + 1e-06
         for p, part in enumerate((re, im)):
             white = (part / den).astype(jnp.bfloat16).astype(jnp.float32) * mask
-            white_ref[2 * w + p] = white
+            white_ref[2 * w + p] = white.astype(jnp.bfloat16)
             picked = jnp.dot(
                 white.astype(jnp.bfloat16), onehot, preferred_element_type=jnp.float32
             )
@@ -249,7 +250,7 @@
     def agc(peer, src_dev):
         return pltpu.make_async_remote_copy(
             src_ref=ag_send,
-            dst_ref=srcspec_ref.at[src_dev],
+            dst_ref=ag_recv.at[src_dev],
             send_sem=ag_send_sem.at[peer],
             recv_sem=ag_recv_sem.at[src_dev],
             device_id={"chan": peer},
@@ -258,12 +259,17 @@
 
     for i in range(1, n_chan):
         agc(lax.rem(mc + i, n_chan), mc).start()
-    srcspec_ref[mc] = ag_send[...]
+    ag_recv[mc] = ag_send[...]
     for i in range(1, n_chan):
         agc(lax.rem(mc + i, n_chan), mc).wait_send()
     for i in range(1, n_chan):
         src = lax.rem(mc + n_chan - i, n_chan)
         agc(src, src).wait_recv()
+
+    for i in range(NWIN * 2):
+        for h in range(halves):
+            srcspec_ref[i, h * per:(h + 1) * per, :] = (
+                ag_recv[i * halves + h, 0:per, :].astype(jnp.bfloat16))
 
 
 def fused_exchange(offsets, record, dead, sources, n_tm, n_chan, bins_dev, first, count):
@@ -274,8 +280,8 @@
     return pl.pallas_call(
         functools.partial(_fused_kernel, n_tm, n_chan, bins_dev, first, count),
         out_shape=(
-            jax.ShapeDtypeStruct((NWIN * 2, bins_dev, channels), jnp.float32),
-            jax.ShapeDtypeStruct((n_chan, 16, nsrc), jnp.float32),
+            jax.ShapeDtypeStruct((NWIN * 2, bins_dev, channels), jnp.bfloat16),
+            jax.ShapeDtypeStruct((NWIN * 2, bins_dev, nsrc), jnp.bfloat16),
         ),
         in_specs=[pl.BlockSpec(memory_space=pltpu.SMEM), vmem, vmem, vmem],
         out_specs=(vmem, vmem),
@@ -302,6 +308,7 @@
             pltpu.VMEM((16, nsrc), jnp.float32),
             pltpu.SemaphoreType.DMA((n_chan,)),
             pltpu.SemaphoreType.DMA((n_chan,)),
+            pltpu.VMEM((n_chan, 16, nsrc), jnp.float32),
         ],
         compiler_params=pltpu.CompilerParams(collective_id=0, has_side_effects=True),
     )(offsets, record, dead, sources)
@@ -320,8 +327,8 @@
 
     per = NWIN * 2 * bins_dev // n_chan
     assert per * n_chan == NWIN * 2 * bins_dev and bins_dev % per == 0 and per <= 16
-    left = source_spec[:, :per].astype(jnp.bfloat16).reshape(NWIN, 2, bins_dev, -1)
-    right = white.astype(jnp.bfloat16).reshape(NWIN, 2, bins_dev, channels)
+    left = source_spec.reshape(NWIN, 2, bins_dev, -1)
+    right = white.reshape(NWIN, 2, bins_dev, channels)
     right_imaginary = jnp.stack([right[:, 1], -right[:, 0]], axis=1)
     real_component = jnp.einsum(
         "wpks,wpkc->ksc", left, right, preferred_element_type=jnp.float32

time: 64.5 us -> 65.2 us (1.011)
  matrix products: 0.81 us -> 2.41 us
  other arithmetic: 1.22 us -> 0.32 us
    slice x1 -> x0, local copies, waits for them, and re-layouts: 0.92 us -> none  [shards(): source_spec[:, :per].astype(jnp.bfloat16).reshape(NWIN, 2, bins_dev, -1)]
    convert_element_type x1 -> x0, other arithmetic: 0.9 us -> none  [shards(): right = white.astype(jnp.bfloat16).reshape(NWIN, 2, bins_dev, channels)]
    dot_general x1, matrix products: 0.41 us -> 1.2 us  [shards(): jnp.einsum('wpks,wpkc->ksc', left, right_imaginary, preferred_element_typ...]
    dot_general x1, matrix products: 0.41 us -> 1.2 us  [shards(): jnp.einsum('wpks,wpkc->ksc', left, right, preferred_element_type=jnp.floa...]
    reshape x2 -> x1, local copies, waits for them, and re-layouts: 0.03 us -> 0.82 us  [shards(): right = white.reshape(NWIN, 2, bins_dev, channels)]
where the time goes in v11:
time: 65.2 us; the launch traced here: 64.9 us
  Pallas kernels  59.6 us (91%)
  local copies, waits for them, and re-layouts  2.49 us (4%)
  matrix products  2.41 us (4%)
    pallas_call x1, Pallas kernels, fused_exchange(): pl.pallas_call(functools.partial(_fused_kernel, n_tm, n_chan, bins_dev, f...  59.6 us
    div x1, local copies, waits for them, and re-layouts, shards(): return jnp.stack([real_component, imaginary_component], axis=1) / NWIN  1.67 us

profile of v11, /device:TPU:1, one launch (start us, length us, event | category | flops | bytes accessed | tf_op | source)
XLA Modules:
  0.0 64.9 jit_solution(6019120396491455404)
XLA Ops:
  0.0 59.6 %shard_map.46 = (bf16[8,20,128]{2,1,0:T(8,128)(2,1)}, bf16[8,20,128]{2,1,0:T(8,128)(2,1)}) custom-call(s32[4]{0:T(128)} %offsets_ref.1, bf16[128,1536]{1,0:T(8,128)(2,1)} %record_ref.1, s32[1,128]{1,0:T(1,128)} %bitcast.16, s32[1,128]{1,0:T(1,128)} %bitcast.17), custom_call_target="tpu_custom_call" | custom-call | tf_op jit(solution)/shard_map/pallas_call | solution.py:280
  59.6 0.8 %copy.6 = bf16[4,2,20,128]{3,0,1,2:T(4,128)(2,1)S(1)} copy(bf16[4,2,20,128]{3,2,1,0:T(8,128)(2,1)} %bitcast.15) | data formatting | bytes 81920 | tf_op jit(solution)/shard_map/reshape | solution.py:331
  60.5 1.2 %convolution_bitcast_fusion = f32[20,1,128,128]{3,2,0,1:T(8,128)S(1)} fusion(bf16[4,1,20,128]{3,0,1,2:T(4,128)(2,1)S(1)} %get-tuple-element.10, bf16[4,1,20,128]{3,0,1,2:T(4,128)(2,1)S(1)} %get-tuple-element.9, bf16[4,2,20,128]{3,2,1,0:T(8,128)(2,1)} %bitcast.13), kind=kOutput, calls=%fused_computation.1 | convolution fusion | flops 5324800 | bytes 1392640 | tf_op jit(solution)/shard_map/wpks,wpkc->ksc/dot_general | solution.py:336
  61.7 1.2 %convolution_bitcast_fusion.1 = f32[20,1,128,128]{3,2,0,1:T(8,128)S(1)} fusion(bf16[4,2,20,128]{3,0,1,2:T(4,128)(2,1)S(1)} %copy.6, bf16[4,2,20,128]{3,2,1,0:T(8,128)(2,1)} %bitcast.14), kind=kOutput, calls=%fused_computation.2 | convolution fusion | flops 5242880 | bytes 1392640 | tf_op jit(solution)/shard_map/wpks,wpkc->ksc/dot_general | solution.py:333
  62.9 0.3 maximum_multiply_fusion
  63.2 1.7 %copy.10 = f32[20,2,128,128]{3,2,1,0:T(8,128)} copy(f32[20,2,128,128]{3,2,0,1:T(8,128)S(1)} %maximum_multiply_fusion) | data formatting | bytes 5242880 | tf_op jit(solution)/shard_map/div | solution.py:339
  (1 shorter events, 0.0 us)

commit v12 on v11

--- a/solution.py
+++ b/solution.py
@@ -33,6 +33,28 @@
     return first, count
 
 
+def _cross_kernel(bins_dev, src_ref, white_ref, rot_ref, out_ref):
+    for k in range(bins_dev):
+        left = src_ref[k].astype(jnp.bfloat16)
+        for p, right_ref in enumerate((white_ref, rot_ref)):
+            out_ref[k, p] = lax.dot_general(
+                left, right_ref[k].astype(jnp.bfloat16), (((0,), (0,)), ((), ())),
+                preferred_element_type=jnp.float32,
+            ) / NWIN
+
+
+def cross_spectra(source_spec, white, rotated):
+    bins_dev, _, nsrc = source_spec.shape
+    channels = white.shape[2]
+    vmem = pl.BlockSpec(memory_space=pltpu.VMEM)
+    return pl.pallas_call(
+        functools.partial(_cross_kernel, bins_dev),
+        out_shape=jax.ShapeDtypeStruct((bins_dev, 2, nsrc, channels), jnp.float32),
+        in_specs=[vmem] * 3,
+        out_specs=vmem,
+    )(source_spec, white, rotated)
+
+
 def _any_of(me, members):
     hit = jnp.bool_(False)
     for m in members:
@@ -42,7 +64,7 @@
 
 def _fused_kernel(n_tm, n_chan, bins_dev, first, count,
                   offsets_ref, record_ref, dead_ref, sources_ref,
-                  white_ref, srcspec_ref,
+                  white_ref, rot_ref, srcspec_ref,
                   ar_ref, ai_ref, c1_ref, c2_ref, x_ref,
                   blocks_ref, lhs, recv, spec, lvl_send, lvl_recv, src_send,
                   a2a_send_sem, a2a_recv_sem, lvl_send_sem, lvl_recv_sem,
@@ -216,7 +238,12 @@
         den = mag + 0.1 * level[w:w + 1, :] + 1e-06
         for p, part in enumerate((re, im)):
             white = (part / den).astype(jnp.bfloat16).astype(jnp.float32) * mask
-            white_ref[2 * w + p] = white.astype(jnp.bfloat16)
+            for k in range(bins_dev):
+                white_ref[k, 2 * w + p:2 * w + p + 1, :] = white[k:k + 1, :]
+                if p == 0:
+                    rot_ref[k, 2 * w + 1:2 * w + 2, :] = -white[k:k + 1, :]
+                else:
+                    rot_ref[k, 2 * w:2 * w + 1, :] = white[k:k + 1, :]
             picked = jnp.dot(
                 white.astype(jnp.bfloat16), onehot, preferred_element_type=jnp.float32
             )
@@ -268,8 +295,9 @@
 
     for i in range(NWIN * 2):
         for h in range(halves):
-            srcspec_ref[i, h * per:(h + 1) * per, :] = (
-                ag_recv[i * halves + h, 0:per, :].astype(jnp.bfloat16))
+            for r in range(per):
+                k = h * per + r
+                srcspec_ref[k, i:i + 1, :] = ag_recv[i * halves + h, r:r + 1, :]
 
 
 def fused_exchange(offsets, record, dead, sources, n_tm, n_chan, bins_dev, first, count):
@@ -280,11 +308,12 @@
     return pl.pallas_call(
         functools.partial(_fused_kernel, n_tm, n_chan, bins_dev, first, count),
         out_shape=(
-            jax.ShapeDtypeStruct((NWIN * 2, bins_dev, channels), jnp.bfloat16),
-            jax.ShapeDtypeStruct((NWIN * 2, bins_dev, nsrc), jnp.bfloat16),
+            jax.ShapeDtypeStruct((bins_dev, NWIN * 2, channels), jnp.float32),
+            jax.ShapeDtypeStruct((bins_dev, NWIN * 2, channels), jnp.float32),
+            jax.ShapeDtypeStruct((bins_dev, NWIN * 2, nsrc), jnp.float32),
         ),
         in_specs=[pl.BlockSpec(memory_space=pltpu.SMEM), vmem, vmem, vmem],
-        out_specs=(vmem, vmem),
+        out_specs=(vmem, vmem, vmem),
         scratch_shapes=[
             pltpu.VMEM((SLOTS, n_tm, span), jnp.float32),
             pltpu.VMEM((SLOTS, n_tm, span), jnp.float32),
@@ -320,23 +349,13 @@
     bins_dev = F // n_tm
     channels, span = record.shape
     first, count = window_plan(n_tm, span)
-    white, source_spec = fused_exchange(
+    per = NWIN * 2 * bins_dev // n_chan
+    assert per * n_chan == NWIN * 2 * bins_dev and bins_dev % per == 0 and per <= 16
+    white, rotated, source_spec = fused_exchange(
         offsets, record, dead_mask.reshape(1, channels), sources.reshape(1, -1),
         n_tm, n_chan, bins_dev, first, count
     )
-
-    per = NWIN * 2 * bins_dev // n_chan
-    assert per * n_chan == NWIN * 2 * bins_dev and bins_dev % per == 0 and per <= 16
-    left = source_spec.reshape(NWIN, 2, bins_dev, -1)
-    right = white.reshape(NWIN, 2, bins_dev, channels)
-    right_imaginary = jnp.stack([right[:, 1], -right[:, 0]], axis=1)
-    real_component = jnp.einsum(
-        "wpks,wpkc->ksc", left, right, preferred_element_type=jnp.float32
-    )
-    imaginary_component = jnp.einsum(
-        "wpks,wpkc->ksc", left, right_imaginary, preferred_element_type=jnp.float32
-    )
-    return jnp.stack([real_component, imaginary_component], axis=1) / NWIN
+    return cross_spectra(source_spec, white, rotated)
 
 
 def solution(mesh):

time: 65.2 us -> 62.9 us (0.965)
  Pallas kernels: 59.6 us -> 62.7 us
  local copies, waits for them, and re-layouts: 2.49 us -> 0 us
  matrix products: 2.41 us -> 0 us
    pallas_call x0 -> x1, Pallas kernels: none -> 3.01 us  [cross_spectra(): pl.pallas_call(functools.partial(_cross_kernel, bins_dev), out_shape=jax....]
    dot_general x2 -> x0, matrix products: 2.41 us -> none  [the longest x1 1.2 us: shards(): jnp.einsum('wpks,wpkc->ksc', left, right_imaginary, preferred_element_typ...]
    div x1 -> x0, local copies, waits for them, and re-layouts: 1.67 us -> none  [shards(): return jnp.stack([real_component, imaginary_component], axis=1) / NWIN]
    reshape x1 -> x0, local copies, waits for them, and re-layouts: 0.82 us -> none  [shards(): right = white.reshape(NWIN, 2, bins_dev, channels)]
where the time goes in v12:
time: 62.9 us; the launch traced here: 62.7 us
  Pallas kernels  62.7 us (100%)
    pallas_call x1, Pallas kernels, fused_exchange(): pl.pallas_call(functools.partial(_fused_kernel, n_tm, n_chan, bins_dev, f...  59.7 us
    pallas_call x1, Pallas kernels, cross_spectra(): pl.pallas_call(functools.partial(_cross_kernel, bins_dev), out_shape=jax....  3.01 us

profile of v12, /device:TPU:1, one launch (start us, length us, event | category | flops | bytes accessed | tf_op | source)
XLA Modules:
  0.0 62.7 jit_solution(1856844967875424867)
XLA Ops:
  0.0 59.7 %shard_map.46 = (f32[20,8,128]{2,1,0:T(8,128)}, f32[20,8,128]{2,1,0:T(8,128)}, f32[20,8,128]{2,1,0:T(8,128)}) custom-call(s32[4]{0:T(128)} %offsets_ref.1, bf16[128,1536]{1,0:T(8,128)(2,1)} %record_ref.1, s32[1,128]{1,0:T(1,128)} %bitcast.2, s32[1,128]{1,0:T(1,128)} %bitcast.3), custom_call_target="tpu_custom_call" | custom-call | tf_op jit(solution)/shard_map/pallas_call | solution.py:308
  59.7 3.0 %shard_map.47 = f32[20,2,128,128]{3,2,1,0:T(8,128)} custom-call(f32[20,8,128]{2,1,0:T(8,128)} %get-tuple-element.8.src_ref, f32[20,8,128]{2,1,0:T(8,128)} %get-tuple-element.9.white_ref, f32[20,8,128]{2,1,0:T(8,128)} %get-tuple-element.10.rot_ref), custom_call_target="tpu_custom_call" | custom-call | tf_op jit(solution)/shard_map/pallas_call | solution.py:50

commit v13 on v12

--- a/solution.py
+++ b/solution.py
@@ -131,7 +131,7 @@
         c1 = c1_ref[slot]
         c2 = c2_ref[slot]
         for dd in range(group):
-            d = lax.rem(me + g * group + dd, n_tm)
+            d = lax.rem(me + n_tm - (g * group + dd), n_tm)
             ar = ar_ref[slot, pl.ds(d, 1), :]
             ai = ai_ref[slot, pl.ds(d, 1), :]
             lhs[dd * rows:(dd + 1) * rows, :] = ar * c1 + ai * c2
@@ -140,14 +140,14 @@
             preferred_element_type=jnp.float32,
         )
         for dd in range(group):
-            d = lax.rem(me + g * group + dd, n_tm)
+            d = lax.rem(me + n_tm - (g * group + dd), n_tm)
             blocks_ref[d, slot] = res[dd * rows:(dd + 1) * rows, :]
 
     def send(g, slot):
         for dd in range(group):
             if g == 0 and dd == 0:
                 continue
-            a2a(lax.rem(me + g * group + dd, n_tm), slot, me).start()
+            a2a(lax.rem(me + n_tm - (g * group + dd), n_tm), slot, me).start()
 
     for g in range(n_tm // group):
         compute(g, 0)

time: 62.9 us -> 63.2 us (level)
  no operation moved by 1% of the time
where the time goes in v13:
time: 63.2 us; the launch traced here: 62.5 us
  Pallas kernels  62.5 us (99%)
    pallas_call x1, Pallas kernels, fused_exchange(): pl.pallas_call(functools.partial(_fused_kernel, n_tm, n_chan, bins_dev, f...  59.5 us
    pallas_call x1, Pallas kernels, cross_spectra(): pl.pallas_call(functools.partial(_cross_kernel, bins_dev), out_shape=jax....  3.01 us

profile of v13, /device:TPU:1, one launch (start us, length us, event | category | flops | bytes accessed | tf_op | source)
XLA Modules:
  0.0 62.5 jit_solution(5770624498305974403)
XLA Ops:
  0.0 59.5 %shard_map.46 = (f32[20,8,128]{2,1,0:T(8,128)}, f32[20,8,128]{2,1,0:T(8,128)}, f32[20,8,128]{2,1,0:T(8,128)}) custom-call(s32[4]{0:T(128)} %offsets_ref.1, bf16[128,1536]{1,0:T(8,128)(2,1)} %record_ref.1, s32[1,128]{1,0:T(1,128)} %bitcast.2, s32[1,128]{1,0:T(1,128)} %bitcast.3), custom_call_target="tpu_custom_call" | custom-call | tf_op jit(solution)/shard_map/pallas_call | solution.py:308
  59.5 3.0 %shard_map.47 = f32[20,2,128,128]{3,2,1,0:T(8,128)} custom-call(f32[20,8,128]{2,1,0:T(8,128)} %get-tuple-element.8.src_ref, f32[20,8,128]{2,1,0:T(8,128)} %get-tuple-element.9.white_ref, f32[20,8,128]{2,1,0:T(8,128)} %get-tuple-element.10.rot_ref), custom_call_target="tpu_custom_call" | custom-call | tf_op jit(solution)/shard_map/pallas_call | solution.py:50

commit v14 on v12

--- a/solution.py
+++ b/solution.py
@@ -303,7 +303,7 @@
 def fused_exchange(offsets, record, dead, sources, n_tm, n_chan, bins_dev, first, count):
     channels, span = record.shape
     nsrc = sources.shape[1]
-    group = 8
+    group = 16
     vmem = pl.BlockSpec(memory_space=pltpu.VMEM)
     return pl.pallas_call(
         functools.partial(_fused_kernel, n_tm, n_chan, bins_dev, first, count),

time: 62.9 us -> 61.5 us (0.978)
  Pallas kernels: 62.7 us -> 61.3 us
    pallas_call x1, Pallas kernels: 59.7 us -> 58.3 us  [fused_exchange(): pl.pallas_call(functools.partial(_fused_kernel, n_tm, n_chan, bins_dev, f...]
where the time goes in v14:
time: 61.5 us; the launch traced here: 61.3 us
  Pallas kernels  61.3 us (100%)
    pallas_call x1, Pallas kernels, fused_exchange(): pl.pallas_call(functools.partial(_fused_kernel, n_tm, n_chan, bins_dev, f...  58.3 us
    pallas_call x1, Pallas kernels, cross_spectra(): pl.pallas_call(functools.partial(_cross_kernel, bins_dev), out_shape=jax....  3.01 us

profile of v14, /device:TPU:1, one launch (start us, length us, event | category | flops | bytes accessed | tf_op | source)
XLA Modules:
  0.0 61.3 jit_solution(15741353475974496404)
XLA Ops:
  0.0 58.3 %shard_map.46 = (f32[20,8,128]{2,1,0:T(8,128)}, f32[20,8,128]{2,1,0:T(8,128)}, f32[20,8,128]{2,1,0:T(8,128)}) custom-call(s32[4]{0:T(128)} %offsets_ref.1, bf16[128,1536]{1,0:T(8,128)(2,1)} %record_ref.1, s32[1,128]{1,0:T(1,128)} %bitcast.2, s32[1,128]{1,0:T(1,128)} %bitcast.3), custom_call_target="tpu_custom_call" | custom-call | tf_op jit(solution)/shard_map/pallas_call | solution.py:308
  58.3 3.0 %shard_map.47 = f32[20,2,128,128]{3,2,1,0:T(8,128)} custom-call(f32[20,8,128]{2,1,0:T(8,128)} %get-tuple-element.8.src_ref, f32[20,8,128]{2,1,0:T(8,128)} %get-tuple-element.9.white_ref, f32[20,8,128]{2,1,0:T(8,128)} %get-tuple-element.10.rot_ref), custom_call_target="tpu_custom_call" | custom-call | tf_op jit(solution)/shard_map/pallas_call | solution.py:50

commit v15 on v14

--- a/solution.py
+++ b/solution.py
@@ -303,7 +303,7 @@
 def fused_exchange(offsets, record, dead, sources, n_tm, n_chan, bins_dev, first, count):
     channels, span = record.shape
     nsrc = sources.shape[1]
-    group = 16
+    group = 32
     vmem = pl.BlockSpec(memory_space=pltpu.VMEM)
     return pl.pallas_call(
         functools.partial(_fused_kernel, n_tm, n_chan, bins_dev, first, count),

time: 61.5 us -> 62 us (level)
  no operation moved by 1% of the time
where the time goes in v15:
time: 62 us; the launch traced here: 61.8 us
  Pallas kernels  61.8 us (100%)
    pallas_call x1, Pallas kernels, fused_exchange(): pl.pallas_call(functools.partial(_fused_kernel, n_tm, n_chan, bins_dev, f...  58.8 us
    pallas_call x1, Pallas kernels, cross_spectra(): pl.pallas_call(functools.partial(_cross_kernel, bins_dev), out_shape=jax....  3.01 us

profile of v15, /device:TPU:1, one launch (start us, length us, event | category | flops | bytes accessed | tf_op | source)
XLA Modules:
  0.0 61.8 jit_solution(11170542140256685924)
XLA Ops:
  0.0 58.8 %shard_map.46 = (f32[20,8,128]{2,1,0:T(8,128)}, f32[20,8,128]{2,1,0:T(8,128)}, f32[20,8,128]{2,1,0:T(8,128)}) custom-call(s32[4]{0:T(128)} %offsets_ref.1, bf16[128,1536]{1,0:T(8,128)(2,1)} %record_ref.1, s32[1,128]{1,0:T(1,128)} %bitcast.2, s32[1,128]{1,0:T(1,128)} %bitcast.3), custom_call_target="tpu_custom_call" | custom-call | tf_op jit(solution)/shard_map/pallas_call | solution.py:308
  58.8 3.0 %shard_map.47 = f32[20,2,128,128]{3,2,1,0:T(8,128)} custom-call(f32[20,8,128]{2,1,0:T(8,128)} %get-tuple-element.8.src_ref, f32[20,8,128]{2,1,0:T(8,128)} %get-tuple-element.9.white_ref, f32[20,8,128]{2,1,0:T(8,128)} %get-tuple-element.10.rot_ref), custom_call_target="tpu_custom_call" | custom-call | tf_op jit(solution)/shard_map/pallas_call | solution.py:50

commit v16 on v14

--- a/solution.py
+++ b/solution.py
@@ -33,25 +33,28 @@
     return first, count
 
 
-def _cross_kernel(bins_dev, src_ref, white_ref, rot_ref, out_ref):
-    for k in range(bins_dev):
-        left = src_ref[k].astype(jnp.bfloat16)
-        for p, right_ref in enumerate((white_ref, rot_ref)):
-            out_ref[k, p] = lax.dot_general(
-                left, right_ref[k].astype(jnp.bfloat16), (((0,), (0,)), ((), ())),
-                preferred_element_type=jnp.float32,
-            ) / NWIN
+def _cross_kernel(src_ref, white_ref, rot_ref, out_ref):
+    left = src_ref[0].astype(jnp.bfloat16)
+    for p, right_ref in enumerate((white_ref, rot_ref)):
+        out_ref[0, p] = lax.dot_general(
+            left, right_ref[0].astype(jnp.bfloat16), (((0,), (0,)), ((), ())),
+            preferred_element_type=jnp.float32,
+        ) / NWIN
 
 
 def cross_spectra(source_spec, white, rotated):
-    bins_dev, _, nsrc = source_spec.shape
+    bins_dev, rows, nsrc = source_spec.shape
     channels = white.shape[2]
-    vmem = pl.BlockSpec(memory_space=pltpu.VMEM)
     return pl.pallas_call(
-        functools.partial(_cross_kernel, bins_dev),
+        _cross_kernel,
         out_shape=jax.ShapeDtypeStruct((bins_dev, 2, nsrc, channels), jnp.float32),
-        in_specs=[vmem] * 3,
-        out_specs=vmem,
+        grid=(bins_dev,),
+        in_specs=[
+            pl.BlockSpec((1, rows, nsrc), lambda k: (k, 0, 0)),
+            pl.BlockSpec((1, rows, channels), lambda k: (k, 0, 0)),
+            pl.BlockSpec((1, rows, channels), lambda k: (k, 0, 0)),
+        ],
+        out_specs=pl.BlockSpec((1, 2, nsrc, channels), lambda k: (k, 0, 0, 0)),
     )(source_spec, white, rotated)
 
 

time: 61.5 us -> 70.2 us (1.14)
  Pallas kernels: 61.3 us -> 69.4 us
    pallas_call x1, Pallas kernels: 3.01 us -> 11.1 us  [cross_spectra(): pl.pallas_call(_cross_kernel, out_shape=jax.ShapeDtypeStruct((bins_dev, 2...]
where the time goes in v16:
time: 70.2 us; the launch traced here: 69.4 us
  Pallas kernels  69.4 us (99%)
    pallas_call x1, Pallas kernels, fused_exchange(): pl.pallas_call(functools.partial(_fused_kernel, n_tm, n_chan, bins_dev, f...  58.3 us
    pallas_call x1, Pallas kernels, cross_spectra(): pl.pallas_call(_cross_kernel, out_shape=jax.ShapeDtypeStruct((bins_dev, 2...  11.1 us

profile of v16, /device:TPU:1, one launch (start us, length us, event | category | flops | bytes accessed | tf_op | source)
XLA Modules:
  0.0 69.4 jit_solution(3271246662981068230)
XLA Ops:
  0.0 58.3 %shard_map.46 = (f32[20,8,128]{2,1,0:T(8,128)}, f32[20,8,128]{2,1,0:T(8,128)}, f32[20,8,128]{2,1,0:T(8,128)}) custom-call(s32[4]{0:T(128)} %offsets_ref.1, bf16[128,1536]{1,0:T(8,128)(2,1)} %record_ref.1, s32[1,128]{1,0:T(1,128)} %bitcast.2, s32[1,128]{1,0:T(1,128)} %bitcast.3), custom_call_target="tpu_custom_call" | custom-call | tf_op jit(solution)/shard_map/pallas_call | solution.py:311
  58.3 11.1 %shard_map.47 = f32[20,2,128,128]{3,2,1,0:T(8,128)} custom-call(f32[20,8,128]{2,1,0:T(8,128)} %get-tuple-element.8.src_ref, f32[20,8,128]{2,1,0:T(8,128)} %get-tuple-element.9.white_ref, f32[20,8,128]{2,1,0:T(8,128)} %get-tuple-element.10.rot_ref), custom_call_target="tpu_custom_call" | custom-call | tf_op jit(solution)/shard_map/pallas_call | solution.py:48

commit v17 on v14

--- a/solution.py
+++ b/solution.py
@@ -155,8 +155,9 @@
             pl.semaphore_wait(barrier, n_tm - 1 + n_chan - 1)
         send(g, 0)
 
-        @pl.when(me_two)
-        def _():
+    @pl.when(me_two)
+    def _():
+        for g in range(n_tm // group):
             compute(g, 1)
             send(g, 1)
 

time: 61.5 us -> 62.2 us (1.011)
  no operation moved by 1% of the time
where the time goes in v17:
time: 62.2 us; the launch traced here: 61.8 us
  Pallas kernels  61.8 us (99%)
    pallas_call x1, Pallas kernels, fused_exchange(): pl.pallas_call(functools.partial(_fused_kernel, n_tm, n_chan, bins_dev, f...  58.8 us
    pallas_call x1, Pallas kernels, cross_spectra(): pl.pallas_call(functools.partial(_cross_kernel, bins_dev), out_shape=jax....  3.01 us

profile of v17, /device:TPU:1, one launch (start us, length us, event | category | flops | bytes accessed | tf_op | source)
XLA Modules:
  0.0 61.8 jit_solution(7123598056285498610)
XLA Ops:
  0.0 58.8 %shard_map.46 = (f32[20,8,128]{2,1,0:T(8,128)}, f32[20,8,128]{2,1,0:T(8,128)}, f32[20,8,128]{2,1,0:T(8,128)}) custom-call(s32[4]{0:T(128)} %offsets_ref.1, bf16[128,1536]{1,0:T(8,128)(2,1)} %record_ref.1, s32[1,128]{1,0:T(1,128)} %bitcast.2, s32[1,128]{1,0:T(1,128)} %bitcast.3), custom_call_target="tpu_custom_call" | custom-call | tf_op jit(solution)/shard_map/pallas_call | solution.py:309
  58.8 3.0 %shard_map.47 = f32[20,2,128,128]{3,2,1,0:T(8,128)} custom-call(f32[20,8,128]{2,1,0:T(8,128)} %get-tuple-element.8.src_ref, f32[20,8,128]{2,1,0:T(8,128)} %get-tuple-element.9.white_ref, f32[20,8,128]{2,1,0:T(8,128)} %get-tuple-element.10.rot_ref), custom_call_target="tpu_custom_call" | custom-call | tf_op jit(solution)/shard_map/pallas_call | solution.py:50

commit v18 on v14

--- a/solution.py
+++ b/solution.py
@@ -78,11 +78,11 @@
     group = lhs.shape[0] // rows
 
     barrier = pltpu.get_barrier_semaphore()
+    for i in range(1, n_chan):
+        pl.semaphore_signal(barrier, inc=1, device_id={"chan": lax.rem(mc + i, n_chan)},
+                            device_id_type=MESH)
     for i in range(1, n_tm):
         pl.semaphore_signal(barrier, inc=1, device_id={"tm": lax.rem(me + i, n_tm)},
-                            device_id_type=MESH)
-    for i in range(1, n_chan):
-        pl.semaphore_signal(barrier, inc=1, device_id={"chan": lax.rem(mc + i, n_chan)},
                             device_id_type=MESH)
 
     span = record_ref.shape[1]

time: 61.5 us -> 61.9 us (level)
  no operation moved by 1% of the time
where the time goes in v18:
time: 61.9 us; the launch traced here: 61.2 us
  Pallas kernels  61.2 us (99%)
    pallas_call x1, Pallas kernels, fused_exchange(): pl.pallas_call(functools.partial(_fused_kernel, n_tm, n_chan, bins_dev, f...  58.2 us
    pallas_call x1, Pallas kernels, cross_spectra(): pl.pallas_call(functools.partial(_cross_kernel, bins_dev), out_shape=jax....  3.01 us

profile of v18, /device:TPU:1, one launch (start us, length us, event | category | flops | bytes accessed | tf_op | source)
XLA Modules:
  0.0 61.2 jit_solution(14301859845398616787)
XLA Ops:
  0.0 58.2 %shard_map.46 = (f32[20,8,128]{2,1,0:T(8,128)}, f32[20,8,128]{2,1,0:T(8,128)}, f32[20,8,128]{2,1,0:T(8,128)}) custom-call(s32[4]{0:T(128)} %offsets_ref.1, bf16[128,1536]{1,0:T(8,128)(2,1)} %record_ref.1, s32[1,128]{1,0:T(1,128)} %bitcast.2, s32[1,128]{1,0:T(1,128)} %bitcast.3), custom_call_target="tpu_custom_call" | custom-call | tf_op jit(solution)/shard_map/pallas_call | solution.py:308
  58.2 3.0 %shard_map.47 = f32[20,2,128,128]{3,2,1,0:T(8,128)} custom-call(f32[20,8,128]{2,1,0:T(8,128)} %get-tuple-element.8.src_ref, f32[20,8,128]{2,1,0:T(8,128)} %get-tuple-element.9.white_ref, f32[20,8,128]{2,1,0:T(8,128)} %get-tuple-element.10.rot_ref), custom_call_target="tpu_custom_call" | custom-call | tf_op jit(solution)/shard_map/pallas_call | solution.py:50

commit v19 on v18

--- a/solution.py
+++ b/solution.py
@@ -238,12 +238,8 @@
         den = mag + 0.1 * level[w:w + 1, :] + 1e-06
         for p, part in enumerate((re, im)):
             white = (part / den).astype(jnp.bfloat16).astype(jnp.float32) * mask
-            for k in range(bins_dev):
-                white_ref[k, 2 * w + p:2 * w + p + 1, :] = white[k:k + 1, :]
-                if p == 0:
-                    rot_ref[k, 2 * w + 1:2 * w + 2, :] = -white[k:k + 1, :]
-                else:
-                    rot_ref[k, 2 * w:2 * w + 1, :] = white[k:k + 1, :]
+            stash = 24 * (2 * w + p)
+            lhs[stash:stash + bins_dev, 0:channels] = white
             picked = jnp.dot(
                 white.astype(jnp.bfloat16), onehot, preferred_element_type=jnp.float32
             )
@@ -263,6 +259,17 @@
     for i in range(1, n_chan):
         rsc(lax.rem(mc + i, n_chan), mc).start()
     rs_recv[mc] = src_send[mc]
+
+    for w in range(NWIN):
+        for p in range(2):
+            stash = 24 * (2 * w + p)
+            white = lhs[stash:stash + bins_dev, 0:channels]
+            for k in range(bins_dev):
+                white_ref[k, 2 * w + p:2 * w + p + 1, :] = white[k:k + 1, :]
+                if p == 0:
+                    rot_ref[k, 2 * w + 1:2 * w + 2, :] = -white[k:k + 1, :]
+                else:
+                    rot_ref[k, 2 * w:2 * w + 1, :] = white[k:k + 1, :]
     for i in range(1, n_chan):
         rsc(lax.rem(mc + i, n_chan), mc).wait_send()
     for i in range(1, n_chan):

time: 61.9 us -> 61.9 us (level)
  no operation moved by 1% of the time
where the time goes in v19:
time: 61.9 us; the launch traced here: 61.2 us
  Pallas kernels  61.2 us (99%)
    pallas_call x1, Pallas kernels, fused_exchange(): pl.pallas_call(functools.partial(_fused_kernel, n_tm, n_chan, bins_dev, f...  58.2 us
    pallas_call x1, Pallas kernels, cross_spectra(): pl.pallas_call(functools.partial(_cross_kernel, bins_dev), out_shape=jax....  3.01 us

profile of v19, /device:TPU:1, one launch (start us, length us, event | category | flops | bytes accessed | tf_op | source)
XLA Modules:
  0.0 61.2 jit_solution(2278857720770628268)
XLA Ops:
  0.0 58.2 %shard_map.46 = (f32[20,8,128]{2,1,0:T(8,128)}, f32[20,8,128]{2,1,0:T(8,128)}, f32[20,8,128]{2,1,0:T(8,128)}) custom-call(s32[4]{0:T(128)} %offsets_ref.1, bf16[128,1536]{1,0:T(8,128)(2,1)} %record_ref.1, s32[1,128]{1,0:T(1,128)} %bitcast.2, s32[1,128]{1,0:T(1,128)} %bitcast.3), custom_call_target="tpu_custom_call" | custom-call | tf_op jit(solution)/shard_map/pallas_call | solution.py:315
  58.2 3.0 %shard_map.47 = f32[20,2,128,128]{3,2,1,0:T(8,128)} custom-call(f32[20,8,128]{2,1,0:T(8,128)} %get-tuple-element.8.src_ref, f32[20,8,128]{2,1,0:T(8,128)} %get-tuple-element.9.white_ref, f32[20,8,128]{2,1,0:T(8,128)} %get-tuple-element.10.rot_ref), custom_call_target="tpu_custom_call" | custom-call | tf_op jit(solution)/shard_map/pallas_call | solution.py:50

commit v20 on v18

--- a/solution.py
+++ b/solution.py
@@ -33,14 +33,23 @@
     return first, count
 
 
-def _cross_kernel(bins_dev, src_ref, white_ref, rot_ref, out_ref):
+def _cross_kernel(bins_dev, src_ref, white_ref, rot_ref, out_ref, buf, sem):
+    copies = []
     for k in range(bins_dev):
+        slot = k % 2
+        if k >= 2:
+            copies[k - 2].wait()
         left = src_ref[k].astype(jnp.bfloat16)
         for p, right_ref in enumerate((white_ref, rot_ref)):
-            out_ref[k, p] = lax.dot_general(
+            buf[slot, p] = lax.dot_general(
                 left, right_ref[k].astype(jnp.bfloat16), (((0,), (0,)), ((), ())),
                 preferred_element_type=jnp.float32,
             ) / NWIN
+        copy = pltpu.make_async_copy(buf.at[slot], out_ref.at[k], sem.at[slot])
+        copy.start()
+        copies.append(copy)
+    for copy in copies[-2:]:
+        copy.wait()
 
 
 def cross_spectra(source_spec, white, rotated):
@@ -51,7 +60,11 @@
         functools.partial(_cross_kernel, bins_dev),
         out_shape=jax.ShapeDtypeStruct((bins_dev, 2, nsrc, channels), jnp.float32),
         in_specs=[vmem] * 3,
-        out_specs=vmem,
+        out_specs=pl.BlockSpec(memory_space=pl.ANY),
+        scratch_shapes=[
+            pltpu.VMEM((2, 2, nsrc, channels), jnp.float32),
+            pltpu.SemaphoreType.DMA((2,)),
+        ],
     )(source_spec, white, rotated)
 
 

time: 61.9 us -> 68.6 us (1.11)
  Pallas kernels: 61.2 us -> 67.9 us
    pallas_call x1, Pallas kernels: 3.01 us -> 9.68 us  [cross_spectra(): pl.pallas_call(functools.partial(_cross_kernel, bins_dev), out_shape=jax....]
where the time goes in v20:
time: 68.6 us; the launch traced here: 67.9 us
  Pallas kernels  67.9 us (99%)
    pallas_call x1, Pallas kernels, fused_exchange(): pl.pallas_call(functools.partial(_fused_kernel, n_tm, n_chan, bins_dev, f...  58.2 us
    pallas_call x1, Pallas kernels, cross_spectra(): pl.pallas_call(functools.partial(_cross_kernel, bins_dev), out_shape=jax....  9.68 us

profile of v20, /device:TPU:1, one launch (start us, length us, event | category | flops | bytes accessed | tf_op | source)
XLA Modules:
  0.0 67.9 jit_solution(1556408109327908659)
XLA Ops:
  0.0 58.2 %shard_map.46 = (f32[20,8,128]{2,1,0:T(8,128)}, f32[20,8,128]{2,1,0:T(8,128)}, f32[20,8,128]{2,1,0:T(8,128)}) custom-call(s32[4]{0:T(128)} %offsets_ref.1, bf16[128,1536]{1,0:T(8,128)(2,1)} %record_ref.1, s32[1,128]{1,0:T(1,128)} %bitcast.2, s32[1,128]{1,0:T(1,128)} %bitcast.3), custom_call_target="tpu_custom_call" | custom-call | tf_op jit(solution)/shard_map/pallas_call | solution.py:321
  58.2 9.7 %shard_map.47 = f32[20,2,128,128]{3,2,1,0:T(8,128)} custom-call(f32[20,8,128]{2,1,0:T(8,128)} %get-tuple-element.8.src_ref, f32[20,8,128]{2,1,0:T(8,128)} %get-tuple-element.9.white_ref, f32[20,8,128]{2,1,0:T(8,128)} %get-tuple-element.10.rot_ref), custom_call_target="tpu_custom_call" | custom-call | tf_op jit(solution)/shard_map/pallas_call | solution.py:59

commit v21 on v18

--- a/solution.py
+++ b/solution.py
@@ -130,13 +130,16 @@
     def compute(g, slot):
         c1 = c1_ref[slot]
         c2 = c2_ref[slot]
-        for dd in range(group):
-            d = lax.rem(me + g * group + dd, n_tm)
-            ar = ar_ref[slot, pl.ds(d, 1), :]
-            ai = ai_ref[slot, pl.ds(d, 1), :]
-            lhs[dd * rows:(dd + 1) * rows, :] = ar * c1 + ai * c2
+        for dd in range(0, group, 2):
+            pair = []
+            for e in range(2):
+                d = lax.rem(me + g * group + dd + e, n_tm)
+                ar = ar_ref[slot, pl.ds(d, 1), :]
+                ai = ai_ref[slot, pl.ds(d, 1), :]
+                pair.append(ar * c1 + ai * c2)
+            lhs[dd * rows:(dd + 2) * rows, :] = jnp.concatenate(pair, axis=0).astype(jnp.bfloat16)
         res = lax.dot_general(
-            lhs[...].astype(jnp.bfloat16), x_ref[slot], (((1,), (1,)), ((), ())),
+            lhs[...], x_ref[slot], (((1,), (1,)), ((), ())),
             preferred_element_type=jnp.float32,
         )
         for dd in range(group):
@@ -321,7 +324,7 @@
             pltpu.VMEM((SLOTS, 2 * bins_dev, span), jnp.float32),
             pltpu.VMEM((SLOTS, channels, span), jnp.bfloat16),
             pltpu.VMEM((n_tm, SLOTS, 2 * bins_dev, channels), jnp.float32),
-            pltpu.VMEM((group * 2 * bins_dev, span), jnp.float32),
+            pltpu.VMEM((group * 2 * bins_dev, span), jnp.bfloat16),
             pltpu.VMEM((n_tm, SLOTS, 2 * bins_dev, channels), jnp.float32),
             pltpu.VMEM((NWIN, 2 * bins_dev, channels), jnp.float32),
             pltpu.VMEM((8, channels), jnp.float32),

time: 61.9 us -> 61.9 us (level)
  no operation moved by 1% of the time
where the time goes in v21:
time: 61.9 us; the launch traced here: 61.3 us
  Pallas kernels  61.3 us (99%)
    pallas_call x1, Pallas kernels, fused_exchange(): pl.pallas_call(functools.partial(_fused_kernel, n_tm, n_chan, bins_dev, f...  58.3 us
    pallas_call x1, Pallas kernels, cross_spectra(): pl.pallas_call(functools.partial(_cross_kernel, bins_dev), out_shape=jax....  3.01 us

profile of v21, /device:TPU:1, one launch (start us, length us, event | category | flops | bytes accessed | tf_op | source)
XLA Modules:
  0.0 61.3 jit_solution(6346025156864372958)
XLA Ops:
  0.0 58.3 %shard_map.46 = (f32[20,8,128]{2,1,0:T(8,128)}, f32[20,8,128]{2,1,0:T(8,128)}, f32[20,8,128]{2,1,0:T(8,128)}) custom-call(s32[4]{0:T(128)} %offsets_ref.1, bf16[128,1536]{1,0:T(8,128)(2,1)} %record_ref.1, s32[1,128]{1,0:T(1,128)} %bitcast.2, s32[1,128]{1,0:T(1,128)} %bitcast.3), custom_call_target="tpu_custom_call" | custom-call | tf_op jit(solution)/shard_map/pallas_call | solution.py:311
  58.3 3.0 %shard_map.47 = f32[20,2,128,128]{3,2,1,0:T(8,128)} custom-call(f32[20,8,128]{2,1,0:T(8,128)} %get-tuple-element.8.src_ref, f32[20,8,128]{2,1,0:T(8,128)} %get-tuple-element.9.white_ref, f32[20,8,128]{2,1,0:T(8,128)} %get-tuple-element.10.rot_ref), custom_call_target="tpu_custom_call" | custom-call | tf_op jit(solution)/shard_map/pallas_call | solution.py:50

commit v22 on v18

--- a/solution.py
+++ b/solution.py
@@ -152,12 +152,17 @@
     for g in range(n_tm // group):
         compute(g, 0)
         if g == 0:
+            @pl.when(me_two)
+            def _():
+                compute(0, 1)
+
             pl.semaphore_wait(barrier, n_tm - 1 + n_chan - 1)
         send(g, 0)
 
         @pl.when(me_two)
         def _():
-            compute(g, 1)
+            if g > 0:
+                compute(g, 1)
             send(g, 1)
 
     recv[me, 0] = blocks_ref[me, 0]

time: 61.9 us -> 61.9 us (level)
  no operation moved by 1% of the time
where the time goes in v22:
time: 61.9 us; the launch traced here: 61.6 us
  Pallas kernels  61.6 us (100%)
    pallas_call x1, Pallas kernels, fused_exchange(): pl.pallas_call(functools.partial(_fused_kernel, n_tm, n_chan, bins_dev, f...  58.6 us
    pallas_call x1, Pallas kernels, cross_spectra(): pl.pallas_call(functools.partial(_cross_kernel, bins_dev), out_shape=jax....  3.01 us

profile of v22, /device:TPU:1, one launch (start us, length us, event | category | flops | bytes accessed | tf_op | source)
XLA Modules:
  0.0 61.6 jit_solution(8375247051348211974)
XLA Ops:
  0.0 58.6 %shard_map.46 = (f32[20,8,128]{2,1,0:T(8,128)}, f32[20,8,128]{2,1,0:T(8,128)}, f32[20,8,128]{2,1,0:T(8,128)}) custom-call(s32[4]{0:T(128)} %offsets_ref.1, bf16[128,1536]{1,0:T(8,128)(2,1)} %record_ref.1, s32[1,128]{1,0:T(1,128)} %bitcast.2, s32[1,128]{1,0:T(1,128)} %bitcast.3), custom_call_target="tpu_custom_call" | custom-call | tf_op jit(solution)/shard_map/pallas_call | solution.py:313
  58.6 3.0 %shard_map.47 = f32[20,2,128,128]{3,2,1,0:T(8,128)} custom-call(f32[20,8,128]{2,1,0:T(8,128)} %get-tuple-element.8.src_ref, f32[20,8,128]{2,1,0:T(8,128)} %get-tuple-element.9.white_ref, f32[20,8,128]{2,1,0:T(8,128)} %get-tuple-element.10.rot_ref), custom_call_target="tpu_custom_call" | custom-call | tf_op jit(solution)/shard_map/pallas_call | solution.py:50

commit v23 on v18

--- a/solution.py
+++ b/solution.py
@@ -196,7 +196,6 @@
         im = spec[w, bins_dev:2 * bins_dev, :]
         mag = jnp.sqrt(re * re + im * im)
         rows.append(jnp.sum(mag, axis=0, keepdims=True))
-    rows.append(jnp.zeros((8 - NWIN, rows[0].shape[1]), jnp.float32))
     lvl_send[...] = jnp.concatenate(rows, axis=0)
 
     def lvl(peer, src_dev):
@@ -324,8 +323,8 @@
             pltpu.VMEM((group * 2 * bins_dev, span), jnp.float32),
             pltpu.VMEM((n_tm, SLOTS, 2 * bins_dev, channels), jnp.float32),
             pltpu.VMEM((NWIN, 2 * bins_dev, channels), jnp.float32),
-            pltpu.VMEM((8, channels), jnp.float32),
-            pltpu.VMEM((n_tm, 8, channels), jnp.float32),
+            pltpu.VMEM((NWIN, channels), jnp.float32),
+            pltpu.VMEM((n_tm, NWIN, channels), jnp.float32),
             pltpu.VMEM((n_chan, 16, nsrc), jnp.float32),
             pltpu.SemaphoreType.DMA((n_tm, SLOTS)),
             pltpu.SemaphoreType.DMA((n_tm, SLOTS)),

time: 61.9 us -> 61.7 us (level)
  no operation moved by 1% of the time
where the time goes in v23:
time: 61.7 us; the launch traced here: 61.5 us
  Pallas kernels  61.5 us (100%)
    pallas_call x1, Pallas kernels, fused_exchange(): pl.pallas_call(functools.partial(_fused_kernel, n_tm, n_chan, bins_dev, f...  58.5 us
    pallas_call x1, Pallas kernels, cross_spectra(): pl.pallas_call(functools.partial(_cross_kernel, bins_dev), out_shape=jax....  3.01 us

profile of v23, /device:TPU:1, one launch (start us, length us, event | category | flops | bytes accessed | tf_op | source)
XLA Modules:
  0.0 61.5 jit_solution(16508226653018085359)
XLA Ops:
  0.0 58.5 %shard_map.46 = (f32[20,8,128]{2,1,0:T(8,128)}, f32[20,8,128]{2,1,0:T(8,128)}, f32[20,8,128]{2,1,0:T(8,128)}) custom-call(s32[4]{0:T(128)} %offsets_ref.1, bf16[128,1536]{1,0:T(8,128)(2,1)} %record_ref.1, s32[1,128]{1,0:T(1,128)} %bitcast.2, s32[1,128]{1,0:T(1,128)} %bitcast.3), custom_call_target="tpu_custom_call" | custom-call | tf_op jit(solution)/shard_map/pallas_call | solution.py:307
  58.5 3.0 %shard_map.47 = f32[20,2,128,128]{3,2,1,0:T(8,128)} custom-call(f32[20,8,128]{2,1,0:T(8,128)} %get-tuple-element.8.src_ref, f32[20,8,128]{2,1,0:T(8,128)} %get-tuple-element.9.white_ref, f32[20,8,128]{2,1,0:T(8,128)} %get-tuple-element.10.rot_ref), custom_call_target="tpu_custom_call" | custom-call | tf_op jit(solution)/shard_map/pallas_call | solution.py:50
